TPU v7x, 128 devices: a whole 4x4x4 slice. The times are simulated.
128 devices in a mesh: row: 8 (over y, core), col: 16 (over x, z).
Axes of the slice: x: 4, y: 4, z: 4, core: 2. Of those that a mesh axis runs over, the one named last changes fastest.
Arguments:
- parent_front: float32 [4, 8, 256, 2, 16, 256], P(None, 'row', None, None, 'col'), may hold values from -6 to 48, as said below
- child_tiles: bfloat16 [128, 64, 256, 256], P(('row', 'col')), may hold values from -6 to 6
- tile_target: int32 [128, 64, 2], replicated, may hold values from 0 to 31, as said below
Outputs:
- factored_front: float32 [4, 8, 256, 2, 16, 256], P(None, 'row', None, None, 'col')
Inputs may be any that keep to these rules, and one draw needn't show every extreme that they name: The leading 6 * 256 rows and columns of parent_front form a symmetric matrix with diagonal entries in 32 to 48 and other entries of magnitude at most 30 / 1536. tile_target[d, s] is the parent tile (row, column) into which tile s of device d is added (device d is mesh row d // 16, column d % 16); rows are 6 or more. Parent tile (I, J) lives on mesh row I % 8, column J % 16. The 64 tiles of one device go to 64 different devices, and one device receives a tile from every device.
All inputs are finite; a program needn't handle non-finite values.
Results may differ from a plain program's by a relative error of at most 0.0003.
Values may be sent and summed in bfloat16 or wider, within the bound.
No kernel may reach another device: no remote copies, remote signals or barrier semaphores. Data moves between devices by JAX's collectives and lax.ppermute only.
A program may use at most 192 MiB of HBM per device.

v0:
```python
import functools

import jax
import jax.numpy as jnp
from jax import lax
from jax.experimental import pallas as pl
from jax.experimental.pallas import tpu as pltpu
from jax.sharding import PartitionSpec as P

PANELS = 6
BOTH = ("row", "col")
F32 = jnp.float32
BF16 = jnp.bfloat16
F16 = jnp.float16
HIGHEST = lax.Precision.HIGHEST


NT = (((1,), (1,)), ((), ()))
NN = (((1,), (0,)), ((), ()))


def dot(a, b, dims, precision=HIGHEST):
    return lax.dot_general(a, b, dims, precision=precision, preferred_element_type=F32)


def split(x):
    high = x.astype(BF16)
    return high, (x - high.astype(F32)).astype(BF16)


def dot3(a, b, dims):
    (ah, al), (bh, bl) = split(a), split(b)
    one = lambda p, q: lax.dot_general(p, q, dims, preferred_element_type=F32)
    return one(ah, bh) + (one(ah, bl) + one(al, bh))


def tile_at(tile, index):
    return pl.ds(pl.multiple_of(index * tile, tile), tile)


def factor_kernel(tile, panels, a_ref, l_ref, w_ref, s_ref, acc_ref):
    rows = lax.broadcasted_iota(jnp.int32, (tile, tile), 0)
    cols = lax.broadcasted_iota(jnp.int32, (tile, tile), 1)
    diag = rows == cols
    eye = jnp.where(diag, 1.0, 0.0).astype(F32)
    weight = jnp.where(rows > cols, 1.0, jnp.where(diag, 0.5, 0.0)).astype(F32)

    at = functools.partial(tile_at, tile)
    place = 0
    for i in range(panels):
        for j in range(i + 1):
            s_ref[i * tile : (i + 1) * tile, j * tile : (j + 1) * tile] = a_ref[
                :, place * tile : (place + 1) * tile
            ]
            place += 1
    l_ref[...] = jnp.zeros_like(l_ref)

    @pl.loop(0, panels)
    def _(k):
        here = at(k)
        block = s_ref[here, here]
        only = jnp.where(diag, block, 0.0)
        down = lax.rsqrt(jnp.sum(only, axis=1, keepdims=True))
        across = lax.rsqrt(jnp.sum(only, axis=0, keepdims=True))
        w_ref[here, :] = jnp.where(diag, down, 0.0)
        acc_ref[...] = block * down * across - eye

        def improve():
            w = w_ref[here, :]
            w_ref[here, :] = w - dot(acc_ref[...] * weight, w, NN)

        def unfinished(state):
            step, worst = state
            return (worst > 1e-5) & (step < 16)

        def refine(state):
            step, _ = state
            improve()
            w = w_ref[here, :]
            left = dot(dot(w, s_ref[here, here], NN), w, NT) - eye
            acc_ref[...] = left
            return step + 1, jnp.max(jnp.abs(left))

        lax.while_loop(unfinished, refine, (jnp.int32(0), jnp.max(jnp.abs(acc_ref[...]))))
        improve()
        l_ref[here, here] = jnp.where(
            rows >= cols, dot(s_ref[here, here], w_ref[here, :], NT), 0.0
        )

        @pl.loop(k + 1, panels)
        def _(i):
            l_ref[at(i), here] = dot3(s_ref[at(i), here], w_ref[here, :], NT)

        @pl.loop(k + 1, panels)
        def _(i):
            @pl.loop(k + 1, i + 1)
            def _(j):
                s_ref[at(i), at(j)] -= dot3(l_ref[at(i), here], l_ref[at(j), here], NT)


def inverse_kernel(tile, panels, l_ref, d_ref, high_ref, low_ref, w_ref, acc_ref):
    at = functools.partial(tile_at, tile)
    w_ref[...] = jnp.zeros_like(w_ref)

    @pl.loop(0, panels)
    def _(i):
        w_ref[at(i), at(i)] = d_ref[at(i), :]

    @pl.loop(1, panels)
    def _(i):
        @pl.loop(0, i)
        def _(j):
            acc_ref[...] = jnp.zeros_like(acc_ref)

            @pl.loop(j, i)
            def _(m):
                acc_ref[...] += dot3(l_ref[at(i), at(m)], w_ref[at(m), at(j)], NN)

            w_ref[at(i), at(j)] = -dot3(d_ref[at(i), :], acc_ref[...], NN)

    @pl.loop(0, panels)
    def _(i):
        high_ref[at(i), :], low_ref[at(i), :] = split(w_ref[at(i), :])


def factor_leading(packed, tile, panels):
    order = tile * panels
    whole = pl.BlockSpec(memory_space=pltpu.VMEM)
    return pl.pallas_call(
        functools.partial(factor_kernel, tile, panels),
        out_shape=[
            jax.ShapeDtypeStruct((order, order), F32),
            jax.ShapeDtypeStruct((order, tile), F32),
        ],
        in_specs=[whole],
        out_specs=[whole] * 2,
        scratch_shapes=[pltpu.VMEM((order, order), F32), pltpu.VMEM((tile, tile), F32)],
        compiler_params=pltpu.CompilerParams(vmem_limit_bytes=32 << 20),
        cost_estimate=pl.CostEstimate(
            flops=12 * order**3, bytes_accessed=8 * order**2, transcendentals=0
        ),
        name="factor",
    )(packed)


def invert_leading(lower, diagonal):
    order, tile = diagonal.shape
    whole = pl.BlockSpec(memory_space=pltpu.VMEM)
    return pl.pallas_call(
        functools.partial(inverse_kernel, tile, order // tile),
        out_shape=[jax.ShapeDtypeStruct((order, order), BF16)] * 2,
        in_specs=[whole] * 2,
        out_specs=[whole] * 2,
        scratch_shapes=[pltpu.VMEM((order, order), F32), pltpu.VMEM((tile, tile), F32)],
        compiler_params=pltpu.CompilerParams(vmem_limit_bytes=36 << 20),
        cost_estimate=pl.CostEstimate(
            flops=12 * order**3, bytes_accessed=8 * order**2, transcendentals=0
        ),
        name="inverse",
    )(lower, diagonal)


def cut_kernel(child_ref, out_ref, wide_ref):
    pieces, deep, stored, tile = out_ref.shape
    lanes = wide_ref.shape[-1]
    for h in range(tile // lanes):
        across = slice(h * lanes, (h + 1) * lanes)
        wide_ref[h] = child_ref[:, :, across].astype(F32).reshape(wide_ref.shape[1:])
        for d in range(pieces):
            for e in range(deep):
                rows = wide_ref[h, pl.ds(d * deep + e, stored, stride=pieces * deep), :]
                out_ref[d, e, :, across] = rows.astype(BF16)


def cut_rows(child, devices):
    stored, tile, _ = child.shape
    deep = tile // devices
    block = 8
    return pl.pallas_call(
        cut_kernel,
        out_shape=jax.ShapeDtypeStruct((devices, deep, stored, tile), BF16),
        grid=(devices // block,),
        in_specs=[pl.BlockSpec((stored, block * deep, tile), lambda g: (0, g, 0))],
        out_specs=pl.BlockSpec((block, deep, stored, tile), lambda g: (g, 0, 0, 0)),
        scratch_shapes=[pltpu.VMEM((tile // 128, stored * block * deep, 128), F32)],
        compiler_params=pltpu.CompilerParams(vmem_limit_bytes=16 << 20),
        cost_estimate=pl.CostEstimate(
            flops=child.size, bytes_accessed=4 * child.size, transcendentals=0
        ),
        name="cut_rows",
    )(child)


def child_sum_kernel(target_ref, child_ref, out_ref):
    @pl.when(pl.program_id(0) == 0)
    def _():
        out_ref[...] = jnp.zeros_like(out_ref)

    sources, pieces, stored, tile = child_ref.shape
    count = sources * stored
    chunk = 256

    @pl.loop(0, out_ref.shape[0] // chunk)
    def _(m):
        rows = pl.ds(pl.multiple_of(m * chunk, chunk), chunk)
        ids = lax.broadcasted_iota(jnp.int32, (chunk, count), 0) + m * chunk
        hot = jnp.where(ids == target_ref[0], 1.0, 0.0).astype(BF16)
        for e in range(pieces):
            right = child_ref[:, e].reshape(count, tile)
            across = slice(e * tile, (e + 1) * tile)
            out_ref[rows, across] += jnp.dot(hot, right, preferred_element_type=F32)


def child_sum(target, child, tiles):
    devices, pieces, stored, tile = child.shape
    block = 8
    return pl.pallas_call(
        child_sum_kernel,
        out_shape=jax.ShapeDtypeStruct((tiles, pieces * tile), F32),
        grid=(devices // block,),
        in_specs=[
            pl.BlockSpec((1, 1, block * stored), lambda g: (g, 0, 0)),
            pl.BlockSpec((block, pieces, stored, tile), lambda g: (g, 0, 0, 0)),
        ],
        out_specs=pl.BlockSpec((tiles, pieces * tile), lambda g: (0, 0)),
        compiler_params=pltpu.CompilerParams(vmem_limit_bytes=24 << 20),
        cost_estimate=pl.CostEstimate(
            flops=2 * tiles * child.size,
            bytes_accessed=2 * child.size + 4 * pieces * tiles * tile,
            transcendentals=0,
        ),
        name="child_sum",
    )(target.reshape(devices // block, 1, block * stored), child)


def whole_call(kernel, name, out_shape, args, scratch=(), scalars=0, limit=32, flops=0):
    whole = pl.BlockSpec(memory_space=pltpu.VMEM)
    moved = sum(x.size * x.dtype.itemsize for x in [*args, *out_shape])
    return pl.pallas_call(
        kernel,
        out_shape=out_shape,
        in_specs=[pl.BlockSpec(memory_space=pltpu.SMEM)] * scalars
        + [whole] * (len(args) - scalars),
        out_specs=[whole] * len(out_shape),
        scratch_shapes=scratch,
        compiler_params=pltpu.CompilerParams(vmem_limit_bytes=limit << 20),
        cost_estimate=pl.CostEstimate(flops=flops, bytes_accessed=moved, transcendentals=0),
        name=name,
    )(*args)


def pack_kernel(panels, base_ref, packed_ref, turned_ref):
    rows, wide, _ = turned_ref.shape
    tile = base_ref.shape[-1]
    cols = base_ref.shape[0] // rows
    deep = packed_ref.shape[0]
    for r in range(rows):
        for k in range(panels):
            turned_ref[r, :, k * tile : (k + 1) * tile] = base_ref[r * cols + k]
    place = 0
    for i in range(panels):
        for j in range(i + 1):
            for e in range(deep):
                at = e * (wide // deep)
                packed_ref[e : e + 1, place * tile : (place + 1) * tile] = base_ref[
                    i * cols + j, at : at + 1, :
                ]
            place += 1


def encode_kernel(panels, sums_ref, base_ref, rows_ref, cols_ref, x_ref):
    rows, wide, order = base_ref.shape
    tile = order // panels
    cols = rows_ref.shape[0] // rows
    slots = sums_ref.shape[0] // rows_ref.shape[0]
    deep = sums_ref.shape[1] // tile
    lrows = wide // deep
    lanes = 128
    lane = lax.broadcasted_iota(jnp.int32, (wide, lanes), 1)
    for r in range(rows):
        powers = jnp.zeros((wide, lanes), F32)
        for k in range(panels):
            first = (r * cols + k) * slots
            child = [
                sums_ref[first : first + lrows, e * tile : (e + 1) * tile] for e in range(deep)
            ]
            x = base_ref[r, :, k * tile : (k + 1) * tile] + jnp.concatenate(child, axis=0)
            top = jnp.maximum(jnp.max(jnp.abs(x), axis=1, keepdims=True), 1e-30)
            power = jnp.floor(jnp.log(top) * 1.4426950408889634) + 1.0
            coded = jnp.round(x * jnp.exp2(15.0 - power))
            coded = jnp.clip(coded, -32767.0, 32767.0)
            powers = jnp.where(lane == k, power, powers)
            for h in range(tile // lanes):
                x_ref[k * (tile // lanes) + h] = coded[:, h * lanes : (h + 1) * lanes]
        x_ref[order // lanes] = powers
        for g in range(order // lanes + 1):
            across = slice(g * lanes, (g + 1) * lanes)
            piece = x_ref[g].astype(jnp.int32).astype(jnp.int16)
            for c in range(cols):
                rows_ref[r * cols + c, :, across] = piece
            for u in range(cols // rows):
                some = x_ref[g, pl.ds(u, wide // 2, stride=2), :]
                some = some.astype(jnp.int32).astype(jnp.int16)
                for m in range(rows):
                    cols_ref[m * cols + u * rows + r, :, across] = some


def spread_rows(raw_ref, out_ref, source, step, count, target, tile):
    lanes = 128
    each = tile // lanes
    groups = raw_ref.shape[0] - 1
    scale = jnp.exp2(raw_ref[groups, pl.ds(source, count, stride=step), :] - 15.0)
    for g in range(groups):
        k = g // each
        x = raw_ref[g, pl.ds(source, count, stride=step), :] * scale[:, k : k + 1]
        out_ref[g, pl.ds(target, count, stride=2), :] = x


def widen(code_ref, raw_ref):
    lanes = 128
    for g in range(raw_ref.shape[0]):
        piece = code_ref[:, :, g * lanes : (g + 1) * lanes].astype(jnp.int32).astype(F32)
        raw_ref[g] = piece.reshape(raw_ref.shape[1:])


def three(ah, al, bh, bl, dims):
    one = lambda p, q: lax.dot_general(p, q, dims, preferred_element_type=F32)
    return one(ah, bh) + (one(ah, bl) + one(al, bh))


def column_kernel(
    tile, panels, code_ref, wh_ref, wl_ref, gh_ref, gl_ref, raw_ref, nat_ref, xh_ref, xl_ref, acc_ref
):
    at = functools.partial(tile_at, tile)
    devices, pieces, _ = code_ref.shape
    lcols = xh_ref.shape[1] // tile
    each = tile // 128
    widen(code_ref, raw_ref)
    for e in range(pieces // lcols):
        for j in range(lcols):
            spread_rows(raw_ref, nat_ref, e * lcols + j, pieces, devices, j * tile + e, tile)
    for k in range(panels):
        x = jnp.concatenate([nat_ref[k * each + h] for h in range(each)], axis=1)
        xh_ref[k], xl_ref[k] = split(x)

    @pl.loop(0, panels)
    def _(step):
        k = panels - 1 - step
        acc_ref[...] = jnp.zeros_like(acc_ref)

        @pl.loop(0, k + 1)
        def _(j):
            acc_ref[...] += three(
                xh_ref[j], xl_ref[j], wh_ref[at(k), at(j)], wl_ref[at(k), at(j)], NT
            )

        xh_ref[k], xl_ref[k] = split(acc_ref[...])

    @pl.loop(0, panels)
    def _(j):
        acc_ref[...] = jnp.zeros_like(acc_ref)

        @pl.loop(j, panels)
        def _(k):
            acc_ref[...] += three(
                xh_ref[k], xl_ref[k], wh_ref[at(k), at(j)], wl_ref[at(k), at(j)], NN
            )

        gh_ref[:, at(j)], gl_ref[:, at(j)] = split(acc_ref[...])


def final_kernel(
    tile,
    panels,
    where_ref,
    code_ref,
    gh_ref,
    gl_ref,
    wh_ref,
    wl_ref,
    top_ref,
    sums_ref,
    front_ref,
    out_ref,
    raw_ref,
    nat_ref,
    bh_ref,
    bl_ref,
    sum_ref,
    add_ref,
):
    lanes = 128
    each = tile // lanes
    devices, pieces, _ = code_ref.shape
    lrows = out_ref.shape[0] // tile
    lcols = out_ref.shape[1] // tile
    deep = pieces // lrows
    my_row = where_ref[0]
    my_col = where_ref[1]
    row_count = where_ref[2]
    factored = my_col < panels
    widen(code_ref, raw_ref)
    for g in range(deep * each):
        sum_ref[g] = sums_ref[:, :, g * lanes : (g + 1) * lanes].reshape(sum_ref.shape[1:])
    bh_ref[...] = gh_ref[...]
    bl_ref[...] = gl_ref[...]

    @pl.when(factored)
    def _():
        bh_ref[:tile] = wh_ref[...]
        bl_ref[:tile] = wl_ref[...]

    @pl.loop(0, lrows)
    def _(i):
        rows = tile_at(tile, i)
        for e in range(deep):
            spread_rows(raw_ref, nat_ref, e * lrows + i, pieces, devices, e, tile)
            for j in range(lcols):
                for h in range(each):
                    add_ref[j * each + h, pl.ds(e, devices, stride=2), :] = sum_ref[
                        e * each + h, pl.ds(j * lrows + i, devices, stride=lcols * lrows), :
                    ]
        x = jnp.concatenate([nat_ref[g] for g in range(nat_ref.shape[0])], axis=1)
        ah, al = split(x)
        leading = my_row + row_count * i < panels
        for j in range(lcols):
            here = slice(j * tile, (j + 1) * tile)
            product = three(ah, al, bh_ref[here], bl_ref[here], NT)
            child = jnp.concatenate([add_ref[j * each + h] for h in range(each)], axis=1)
            value = front_ref[rows, here] + child - product
            cleared = jnp.zeros_like(value)
            if j == 0:
                value = jnp.where(factored, product, value)
                cleared = jnp.where(factored, top_ref[...], cleared)
            out_ref[rows, here] = jnp.where(leading, cleared, value)


def shards(parent_front, child_tiles, tile_target):
    lrows = parent_front.shape[0]
    tile = parent_front.shape[2]
    lcols = parent_front.shape[3]
    row_count = lax.axis_size("row")
    col_count = lax.axis_size("col")
    devices = row_count * col_count
    order = PANELS * tile
    deep = tile // devices
    slots = lrows * lcols
    lanes = 128
    coded = order + lanes
    my_row = lax.axis_index("row")
    my_col = lax.axis_index("col")
    front = parent_front.reshape(lrows * tile, lcols * tile)
    stored = child_tiles.shape[1]
    shape = jax.ShapeDtypeStruct

    base = front[:, :tile].reshape(lrows, devices, deep, tile).transpose(1, 2, 0, 3)
    base = base.reshape(devices, deep * lrows, tile)
    cut = cut_rows(child_tiles.reshape(stored, tile, tile), devices)
    base = lax.all_to_all(base, BOTH, split_axis=0, concat_axis=0, tiled=True)
    packed, base = whole_call(
        functools.partial(pack_kernel, PANELS),
        "pack",
        [
            shape((deep, PANELS * (PANELS + 1) // 2 * tile), F32),
            shape((row_count, deep * lrows, order), F32),
        ],
        [base],
    )
    cut, packed = lax.optimization_barrier((cut, packed))
    packed = lax.all_gather(packed, BOTH, axis=0, tiled=True)
    spread = lax.all_to_all(cut, BOTH, split_axis=0, concat_axis=0, tiled=True)

    rows_all = tile_target[:, :, 0].reshape(-1)
    cols_all = tile_target[:, :, 1].reshape(-1)
    owner = rows_all % row_count * col_count + cols_all % col_count
    target = owner * slots + cols_all // col_count * lrows + rows_all // row_count
    sums = child_sum(target, spread, devices * slots)

    to_rows, to_cols = whole_call(
        functools.partial(encode_kernel, PANELS),
        "encode",
        [
            shape((devices, deep * lrows, coded), jnp.int16),
            shape((devices, deep * lcols, coded), jnp.int16),
        ],
        [sums, base],
        scratch=[pltpu.VMEM((coded // lanes, deep * lrows, lanes), F32)],
    )
    to_owner = sums.reshape(devices, slots, deep * tile).astype(F16)
    packed, to_cols, to_rows, to_owner = lax.optimization_barrier(
        (packed, to_cols, to_rows, to_owner)
    )
    lower, diagonal = factor_leading(packed, tile, PANELS)
    col_side = lax.all_to_all(to_cols, BOTH, split_axis=0, concat_axis=0, tiled=True)
    col_side, lower, diagonal, to_rows = lax.optimization_barrier(
        (col_side, lower, diagonal, to_rows)
    )
    inverse = invert_leading(lower, diagonal)
    row_side = lax.all_to_all(to_rows, BOTH, split_axis=0, concat_axis=0, tiled=True)
    to_owner, row_side = lax.optimization_barrier((to_owner, row_side))
    summed = lax.all_to_all(to_owner, BOTH, split_axis=0, concat_axis=0, tiled=True)

    groups = order // lanes
    right = whole_call(
        functools.partial(column_kernel, tile, PANELS),
        "column",
        [shape((lcols * tile, order), BF16)] * 2,
        [col_side, *inverse],
        scratch=[
            pltpu.VMEM((groups + 1, lcols * tile, lanes), F32),
            pltpu.VMEM((groups, lcols * tile, lanes), F32),
            pltpu.VMEM((PANELS, lcols * tile, tile), BF16),
            pltpu.VMEM((PANELS, lcols * tile, tile), BF16),
            pltpu.VMEM((lcols * tile, tile), F32),
        ],
        flops=12 * lcols * tile * order**2,
    )
    k = jnp.minimum(my_col, PANELS - 1) * tile
    own = [lax.dynamic_slice(w, (k, 0), (tile, order)) for w in inverse]
    top = lax.dynamic_slice(lower, (jnp.minimum(my_row, PANELS - 1) * tile, k), (tile, tile))
    summed = summed.astype(F32)
    where = jnp.stack([my_row, my_col, jnp.int32(row_count)]).astype(jnp.int32)
    (result,) = whole_call(
        functools.partial(final_kernel, tile, PANELS),
        "final",
        [shape(front.shape, F32)],
        [where, row_side, *right, *own, top, summed, front],
        scratch=[
            pltpu.VMEM((groups + 1, lrows * tile, lanes), F32),
            pltpu.VMEM((groups, tile, lanes), F32),
            pltpu.VMEM((lcols * tile, order), BF16),
            pltpu.VMEM((lcols * tile, order), BF16),
            pltpu.VMEM((deep * tile // lanes, lrows * tile * lcols // deep, lanes), F32),
            pltpu.VMEM((lcols * tile // lanes, tile, lanes), F32),
        ],
        scalars=1,
        limit=40,
        flops=6 * lrows * tile * lcols * tile * order,
    )
    return result.reshape(parent_front.shape)


def solution(mesh):
    return jax.shard_map(
        shards,
        mesh=mesh,
        in_specs=(
            P(None, "row", None, None, "col", None),
            P(("row", "col"), None, None, None),
            P(),
        ),
        out_specs=P(None, "row", None, None, "col", None),
        check_vma=False,
    )
```

profile of v0, /device:TPU:1, one launch (start us, length us, event | category | flops | bytes accessed | tf_op | source)
XLA Modules:
  0.0 375.1 jit_solution(10578369551793726122)
XLA Ops:
  6.5 9.0 %reduce = f32[4,256,2,256]{3,2,1,0:T(2,128)} reduce(f32[4,1,256,2,1,256]{5,4,3,2,1,0:T(1,128)} %param.3, f32[]{:T(128)} %constant.71), dimensions={1,4}, to_apply=%param.3.reduce_sub_computation | reduce | bytes 4194308 | tf_op args[0]
  15.6 1.8 copy.32
  17.3 1.1 slice.12
  18.4 1.8 reshape.228
  20.2 1.6 copy.20
  21.9 2.6 reshape.229
  24.5 11.5 %all-to-all-start = ((f32[128,8,256]{2,1,0:T(8,128)}), f32[128,8,256]{2,1,0:T(8,128)S(1)}, u32[]{:S(2)}, u32[]{:S(2)}) async-start(f32[128,8,256]{2,1,0:T(8,128)} %reshape.229), calls=%async_computation | async-start | bytes 2097152 | tf_op jit(solution)/shard_map/all_to_all | solution.py:459
  36.0 3.4 copy-done.1
  39.4 7.3 %cut_rows.1 = bf16[128,2,64,256]{3,2,1,0:T(8,128)(2,1)S(1)} custom-call(bf16[64,256,256]{2,1,0:T(8,128)(2,1)S(1)} %bitcast.14), custom_call_target="tpu_custom_call" | custom-call | flops 4194304 | bytes 16777216 | tf_op jit(solution)/shard_map/cut_rows/pallas_call | solution.py:179
  46.7 3.3 copy-done
  50.0 4.6 %all-to-all-done.base_ref = f32[128,8,256]{2,1,0:T(8,128)S(1)} async-done(((f32[128,8,256]{2,1,0:T(8,128)}), f32[128,8,256]{2,1,0:T(8,128)S(1)}, u32[]{:S(2)}, u32[]{:S(2)}) %all-to-all-start) | async-done | bytes 1048608 | tf_op jit(solution)/shard_map/all_to_all | solution.py:459
  54.7 0.6 copy-done.11
  55.3 6.3 %all-to-all-start.1 = ((bf16[128,2,64,256]{3,2,1,0:T(8,128)(2,1)}), bf16[128,2,64,256]{3,2,1,0:T(8,128)(2,1)}, u32[]{:S(2)}, u32[]{:S(2)}) async-start(bf16[128,2,64,256]{3,2,1,0:T(8,128)(2,1)} %copy-done), calls=%async_computation.1 | async-start | bytes 16777216 | tf_op jit(solution)/shard_map/all_to_all | solution.py:471
  61.8 0.1 reshape_squeeze.8
  62.2 0.5 add_add_fusion.target_ref
  62.7 100.2 %all-to-all-done.1.child_ref = bf16[128,2,64,256]{3,2,1,0:T(8,128)(2,1)} async-done(((bf16[128,2,64,256]{3,2,1,0:T(8,128)(2,1)}), bf16[128,2,64,256]{3,2,1,0:T(8,128)(2,1)}, u32[]{:S(2)}, u32[]{:S(2)}) %all-to-all-start.1) | async-done | bytes 8388640 | tf_op jit(solution)/shard_map/all_to_all | solution.py:471
  162.9 20.9 %child_sum.1.sums_ref = f32[1024,512]{1,0:T(8,128)S(1)} custom-call(s32[16,1,512]{2,1,0:T(1,128)S(1)} %add_add_fusion.target_ref, bf16[128,2,64,256]{3,2,1,0:T(8,128)(2,1)} %all-to-all-done.1.child_ref), custom_call_target="tpu_custom_call" | custom-call | flops 8589934592 | bytes 10485760 | tf_op jit(solution)/shard_map/child_sum/pallas_call | solution.py:217
  183.9 1.1 encode.1
  185.0 1.7 copy-done.3
  186.7 1.2 copy-done.5
  187.9 1.2 convert_bitcast_fusion
  189.2 11.1 %all-gather.3.cloned.1.call-done = f32[128,2,5376]{2,1,0:T(2,128)} async-done(((f32[1,2,5376]{2,1,0:T(2,128)}), f32[128,2,5376]{2,1,0:T(2,128)}) %all-gather.3.cloned.1.call-update) | async-done | bytes 5505040 | tf_op jit(solution)/shard_map/all_gather | solution.py:470
  200.3 7.6 %reshape.232.a_ref = f32[256,5376]{1,0:T(8,128)} reshape(f32[128,2,5376]{2,1,0:T(2,128)} %all-gather.3.cloned.1.call-done) | data formatting | bytes 11010048 | tf_op jit(solution)/shard_map/optimization_barrier | solution.py:490
  207.9 5.7 %all-to-all-start.2 = ((s16[128,4,1664]{2,1,0:T(4,128)(2,1)}), s16[128,4,1664]{2,1,0:T(4,128)(2,1)}, u32[]{:S(2)}, u32[]{:S(2)}) async-start(s16[128,4,1664]{2,1,0:T(4,128)(2,1)} %copy-done.5), calls=%async_computation.2 | async-start | bytes 3407872 | tf_op jit(solution)/shard_map/all_to_all | solution.py:494
  213.5 2.6 copy-done.2
  216.1 42.2 %factor.1 = (f32[1536,1536]{1,0:T(8,128)S(1)}, f32[1536,256]{1,0:T(8,128)S(1)}) custom-call(f32[256,5376]{1,0:T(8,128)S(1)} %copy-done.2), custom_call_target="tpu_custom_call" | custom-call | flops 43486543872 | bytes 18874368 | tf_op jit(solution)/shard_map/factor/pallas_call | solution.py:129
  258.3 3.6 copy-done.12
  261.9 1.1 copy-done.17
  263.1 10.2 %all-to-all-start.3 = ((s16[128,8,1664]{2,1,0:T(8,128)(2,1)}), s16[128,8,1664]{2,1,0:T(8,128)(2,1)}, u32[]{:S(2)}, u32[]{:S(2)}) async-start(s16[128,8,1664]{2,1,0:T(8,128)(2,1)} %copy-done.3), calls=%async_computation.3 | async-start | bytes 6815744 | tf_op jit(solution)/shard_map/all_to_all | solution.py:499
  273.3 1.0 dynamic_slice.11.top_ref
  274.3 1.4 copy-done.18
  275.7 19.9 %inverse.1 = (bf16[1536,1536]{1,0:T(8,128)(2,1)S(1)}, bf16[1536,1536]{1,0:T(8,128)(2,1)S(1)}) custom-call(f32[1536,1536]{1,0:T(8,128)} %copy-done.12, f32[1536,256]{1,0:T(8,128)S(1)} %copy-done.18), custom_call_target="tpu_custom_call" | custom-call | flops 43486543872 | bytes 18874368 | tf_op jit(solution)/shard_map/inverse/pallas_call | solution.py:149
  295.6 1.0 constant_dynamic-slice_fusion
  296.6 2.1 copy-done.7
  298.7 2.2 copy-done.9
  300.9 15.9 %all-to-all-done.3.code_ref = s16[128,8,1664]{2,1,0:T(8,128)(2,1)} async-done(((s16[128,8,1664]{2,1,0:T(8,128)(2,1)}), s16[128,8,1664]{2,1,0:T(8,128)(2,1)}, u32[]{:S(2)}, u32[]{:S(2)}) %all-to-all-start.3) | async-done | bytes 3407904 | tf_op jit(solution)/shard_map/all_to_all | solution.py:499
  316.8 5.2 %all-to-all-start.4 = ((f16[128,8,512]{2,1,0:T(8,128)(2,1)}), f16[128,8,512]{2,1,0:T(8,128)(2,1)}, u32[]{:S(2)}, u32[]{:S(2)}) async-start(f16[128,8,512]{2,1,0:T(8,128)(2,1)} %convert_bitcast_fusion), calls=%async_computation.4 | async-start | bytes 2097152 | tf_op jit(solution)/shard_map/all_to_all | solution.py:501
  322.1 2.3 copy-done.8
  324.4 2.3 copy-done.10
  326.7 20.6 %column.1 = (bf16[512,1536]{1,0:T(8,128)(2,1)S(1)}, bf16[512,1536]{1,0:T(8,128)(2,1)S(1)}) custom-call(s16[128,4,1664]{2,1,0:T(4,128)(2,1)} %all-to-all-done.2.code_ref, bf16[1536,1536]{1,0:T(8,128)(2,1)S(1)} %copy-done.8, bf16[1536,1536]{1,0:T(8,128)(2,1)S(1)} %copy-done.10), custom_call_target="tpu_custom_call" | custom-call | flops 14495514624 | bytes 14286848 | tf_op jit(solution)/shard_map/column/pallas_call | solution.py:239
  347.3 1.1 copy-done.13
  348.4 1.2 copy-done.15
  349.6 1.7 convert_element_type.11.sums_ref
  351.3 0.3 copy-done.14
  351.6 1.4 copy-done.16
  353.0 9.2 %final.1 = f32[1024,512]{1,0:T(8,128)S(1)} custom-call(s32[3]{0:T(128)S(1)} %pad_add_fusion.where_ref, s16[128,8,1664]{2,1,0:T(8,128)(2,1)} %all-to-all-done.3.code_ref, bf16[512,1536]{1,0:T(8,128)(2,1)S(1)} %copy-done.14, bf16[512,1536]{1,0:T(8,128)(2,1)S(1)} %copy-done.16, bf16[256,1536]{1,0:T(8,128)(2,1)S(1)} %copy-done.6, ...), custom_call_target="tpu_custom_call" | custom-call | flops 4831838208 | bytes 14680076 | tf_op jit(solution)/shard_map/final/pallas_call | solution.py:239
  362.2 1.3 copy-done.4
  363.6 4.7 %reshape.233 = f32[4,1,256,2,1,256]{5,4,3,2,1,0:T(1,128)} reshape(f32[1024,512]{1,0:T(8,128)} %copy-done.4) | data formatting | bytes 4194304 | tf_op jit(solution)/shard_map/reshape | solution.py:540
  (32 shorter events, 0.6 us)
Async XLA Ops:
  24.5 30.1 %all-to-all-start = ((f32[128,8,256]{2,1,0:T(8,128)}), f32[128,8,256]{2,1,0:T(8,128)S(1)}, u32[]{:S(2)}, u32[]{:S(2)}) async-start(f32[128,8,256]{2,1,0:T(8,128)} %reshape.229), calls=%async_computation | async-start | bytes 2097152 | tf_op jit(solution)/shard_map/all_to_all | solution.py:459
  36.0 164.3 %all-gather.3.cloned.1.call-start = ((), (), s32[]{:S(2)}) async-start(), calls=%async_computation.5 | async-start | bytes 5548032 | tf_op jit(solution)/shard_map/all_gather | solution.py:470
  36.0 3.4 copy-start.1
  46.7 3.3 copy-start
  54.7 0.6 copy-start.11
  55.3 6.3 %copy-start.19 = (s32[128,64,2]{0,2,1:T(2,128)S(1)}, s32[128,64,2]{0,2,1:T(2,128)}, u32[]{:S(2)}) copy-start(s32[128,64,2]{0,2,1:T(2,128)} %param.5) | copy-start | bytes 196612
  55.3 107.6 %all-to-all-start.1 = ((bf16[128,2,64,256]{3,2,1,0:T(8,128)(2,1)}), bf16[128,2,64,256]{3,2,1,0:T(8,128)(2,1)}, u32[]{:S(2)}, u32[]{:S(2)}) async-start(bf16[128,2,64,256]{3,2,1,0:T(8,128)(2,1)} %copy-done), calls=%async_computation.1 | async-start | bytes 16777216 | tf_op jit(solution)/shard_map/all_to_all | solution.py:471
  185.0 1.7 copy-start.3
  186.7 1.2 copy-start.5
  207.9 55.2 %all-to-all-start.2 = ((s16[128,4,1664]{2,1,0:T(4,128)(2,1)}), s16[128,4,1664]{2,1,0:T(4,128)(2,1)}, u32[]{:S(2)}, u32[]{:S(2)}) async-start(s16[128,4,1664]{2,1,0:T(4,128)(2,1)} %copy-done.5), calls=%async_computation.2 | async-start | bytes 3407872 | tf_op jit(solution)/shard_map/all_to_all | solution.py:494
  213.5 2.6 copy-start.2
  258.3 3.7 copy-start.12
  261.9 1.1 copy-start.17
  263.1 53.8 %all-to-all-start.3 = ((s16[128,8,1664]{2,1,0:T(8,128)(2,1)}), s16[128,8,1664]{2,1,0:T(8,128)(2,1)}, u32[]{:S(2)}, u32[]{:S(2)}) async-start(s16[128,8,1664]{2,1,0:T(8,128)(2,1)} %copy-done.3), calls=%async_computation.3 | async-start | bytes 6815744 | tf_op jit(solution)/shard_map/all_to_all | solution.py:499
  274.2 1.4 copy-start.18
  296.6 2.1 copy-start.7
  298.7 2.2 copy-start.9
  316.8 32.8 %all-to-all-start.4 = ((f16[128,8,512]{2,1,0:T(8,128)(2,1)}), f16[128,8,512]{2,1,0:T(8,128)(2,1)}, u32[]{:S(2)}, u32[]{:S(2)}) async-start(f16[128,8,512]{2,1,0:T(8,128)(2,1)} %convert_bitcast_fusion), calls=%async_computation.4 | async-start | bytes 2097152 | tf_op jit(solution)/shard_map/all_to_all | solution.py:501
  322.0 2.3 copy-start.8
  324.4 2.3 copy-start.10
  347.3 1.1 copy-start.13
  348.4 1.2 copy-start.15
  349.6 1.7 copy-start.6
  349.6 2.0 copy-start.14
  351.6 1.4 copy-start.16
  362.2 1.4 copy-start.4
Sparse Core Ops, SparseCore 0:
  55.4 144.7 all-gather.2
where the time goes:
time: 376 us; the launch traced here: 375 us
  waiting for transfers between devices  132 us (35%)
  Pallas kernels  121 us (32%)
  local copies, waits for them, and re-layouts  56.9 us (15%)
  starting transfers between devices  38.9 us (10%)
  between operations  13.7 us (4%)
  other arithmetic  12.5 us (3%)
    all_to_all x1, waiting for transfers between devices, shards(): spread = lax.all_to_all(cut, BOTH, split_axis=0, concat_axis=0, tiled=True)  100 us
    pallas_call x1, Pallas kernels, factor_leading(): pl.pallas_call(functools.partial(factor_kernel, tile, panels), out_shape=...  42.2 us
    unnamed x41, local copies, waits for them, and re-layouts  35 us
    pallas_call x4, Pallas kernels, whole_call(): pl.pallas_call(kernel, out_shape=out_shape, in_specs=[pl.BlockSpec(memory...  31 us
    pallas_call x1, Pallas kernels, child_sum(): pl.pallas_call(child_sum_kernel, out_shape=jax.ShapeDtypeStruct((tiles, p...  20.9 us
    pallas_call x1, Pallas kernels, invert_leading(): pl.pallas_call(functools.partial(inverse_kernel, tile, order // tile), ou...  19.9 us
    all_to_all x1, waiting for transfers between devices, shards(): lax.all_to_all(to_rows, BOTH, split_axis=0, concat_axis=0, tiled=True)  15.9 us
    all_to_all x1, starting transfers between devices, shards(): base = lax.all_to_all(base, BOTH, split_axis=0, concat_axis=0, tiled=True)  11.5 us
  transfers between devices with their start and end apart: 6, of which 4 were waited for; matrix products, arithmetic and copies ran while one was open for 1% of the time, Pallas kernels for 30%

commit v1 on v0

v1 whole, which is shorter than its diff:
```python
import functools

import jax
import jax.numpy as jnp
from jax import lax
from jax.experimental import pallas as pl
from jax.experimental.pallas import tpu as pltpu
from jax.sharding import PartitionSpec as P

PANELS = 6
BOTH = ("row", "col")
F32 = jnp.float32
BF16 = jnp.bfloat16
F16 = jnp.float16
HIGHEST = lax.Precision.HIGHEST


NT = (((1,), (1,)), ((), ()))
NN = (((1,), (0,)), ((), ()))


def dot(a, b, dims, precision=HIGHEST):
    return lax.dot_general(a, b, dims, precision=precision, preferred_element_type=F32)


def split(x):
    high = x.astype(BF16)
    return high, (x - high.astype(F32)).astype(BF16)


def three(ah, al, bh, bl, dims):
    (left,), (right,) = dims[0]
    return lax.dot_general(
        jnp.concatenate([ah, ah, al], axis=left),
        jnp.concatenate([bh, bl, bh], axis=right),
        dims,
        preferred_element_type=F32,
    )


def dot3(a, b, dims):
    return three(*split(a), *split(b), dims)


def tile_at(tile, index):
    return pl.ds(pl.multiple_of(index * tile, tile), tile)


def leading_kernel(
    tile,
    panels,
    places,
    where_ref,
    a_ref,
    high_ref,
    low_ref,
    own_high_ref,
    own_low_ref,
    top_ref,
    l_ref,
    s_ref,
    d_ref,
    acc_ref,
):
    rows = lax.broadcasted_iota(jnp.int32, (tile, tile), 0)
    cols = lax.broadcasted_iota(jnp.int32, (tile, tile), 1)
    diag = rows == cols
    eye = jnp.where(diag, 1.0, 0.0).astype(F32)
    weight = jnp.where(rows > cols, 1.0, jnp.where(diag, 0.5, 0.0)).astype(F32)

    at = functools.partial(tile_at, tile)
    for (i, j), (down, across) in places.items():
        s_ref[i * tile : (i + 1) * tile, j * tile : (j + 1) * tile] = a_ref[
            down * tile : (down + 1) * tile, across * tile : (across + 1) * tile
        ]
    l_ref[...] = jnp.zeros_like(l_ref)

    @pl.loop(0, panels)
    def _(k):
        here = at(k)
        block = s_ref[here, here]
        only = jnp.where(diag, block, 0.0)
        down = lax.rsqrt(jnp.sum(only, axis=1, keepdims=True))
        across = lax.rsqrt(jnp.sum(only, axis=0, keepdims=True))
        d_ref[here, :] = jnp.where(diag, down, 0.0)
        acc_ref[...] = block * down * across - eye

        def improve():
            w = d_ref[here, :]
            d_ref[here, :] = w - dot(acc_ref[...] * weight, w, NN)

        def unfinished(state):
            step, worst = state
            return (worst > 1e-5) & (step < 16)

        def refine(state):
            step, _ = state
            improve()
            w = d_ref[here, :]
            left = dot(dot(w, s_ref[here, here], NN), w, NT) - eye
            acc_ref[...] = left
            return step + 1, jnp.max(jnp.abs(left))

        lax.while_loop(unfinished, refine, (jnp.int32(0), jnp.max(jnp.abs(acc_ref[...]))))
        improve()
        l_ref[here, here] = jnp.where(
            rows >= cols, dot(s_ref[here, here], d_ref[here, :], NT), 0.0
        )

        @pl.loop(k + 1, panels)
        def _(i):
            l_ref[at(i), here] = dot3(s_ref[at(i), here], d_ref[here, :], NT)

        @pl.loop(k + 1, panels)
        def _(i):
            @pl.loop(k + 1, i + 1)
            def _(j):
                s_ref[at(i), at(j)] -= dot3(l_ref[at(i), here], l_ref[at(j), here], NT)

    w_ref = s_ref
    w_ref[...] = jnp.zeros_like(w_ref)

    @pl.loop(0, panels)
    def _(i):
        w_ref[at(i), at(i)] = d_ref[at(i), :]

    @pl.loop(1, panels)
    def _(i):
        @pl.loop(0, i)
        def _(j):
            acc_ref[...] = jnp.zeros_like(acc_ref)

            @pl.loop(j, i)
            def _(m):
                acc_ref[...] += dot3(l_ref[at(i), at(m)], w_ref[at(m), at(j)], NN)

            w_ref[at(i), at(j)] = -dot3(d_ref[at(i), :], acc_ref[...], NN)

    @pl.loop(0, panels)
    def _(i):
        high_ref[at(i), :], low_ref[at(i), :] = split(w_ref[at(i), :])

    r = jnp.minimum(where_ref[0], panels - 1)
    c = jnp.minimum(where_ref[1], panels - 1)
    own_high_ref[...], own_low_ref[...] = split(w_ref[at(c), :])
    top_ref[...] = l_ref[at(r), at(c)]


def cut_kernel(child_ref, out_ref, wide_ref):
    pieces, deep, stored, tile = out_ref.shape
    lanes = wide_ref.shape[-1]
    for h in range(tile // lanes):
        across = slice(h * lanes, (h + 1) * lanes)
        wide_ref[h] = child_ref[:, :, across].astype(F32).reshape(wide_ref.shape[1:])
        for d in range(pieces):
            for e in range(deep):
                rows = wide_ref[h, pl.ds(d * deep + e, stored, stride=pieces * deep), :]
                out_ref[d, e, :, across] = rows.astype(BF16)


def cut_rows(child, devices):
    stored, tile, _ = child.shape
    deep = tile // devices
    block = 8
    return pl.pallas_call(
        cut_kernel,
        out_shape=jax.ShapeDtypeStruct((devices, deep, stored, tile), BF16),
        grid=(devices // block,),
        in_specs=[pl.BlockSpec((stored, block * deep, tile), lambda g: (0, g, 0))],
        out_specs=pl.BlockSpec((block, deep, stored, tile), lambda g: (g, 0, 0, 0)),
        scratch_shapes=[pltpu.VMEM((tile // 128, stored * block * deep, 128), F32)],
        compiler_params=pltpu.CompilerParams(vmem_limit_bytes=58 << 20),
        cost_estimate=pl.CostEstimate(
            flops=child.size, bytes_accessed=4 * child.size, transcendentals=0
        ),
        name="cut_rows",
    )(child)


def child_sum_kernel(target_ref, child_ref, out_ref):
    @pl.when(pl.program_id(0) == 0)
    def _():
        out_ref[...] = jnp.zeros_like(out_ref)

    sources, pieces, stored, tile = child_ref.shape
    count = sources * stored
    ids = lax.broadcasted_iota(jnp.int32, (out_ref.shape[0], count), 0)
    hot = jnp.where(ids == target_ref[0], 1.0, 0.0).astype(BF16)
    for e in range(pieces):
        right = child_ref[:, e].reshape(count, tile)
        out_ref[:, e * tile : (e + 1) * tile] += jnp.dot(hot, right, preferred_element_type=F32)


def child_sum(target, child, tiles):
    devices, pieces, stored, tile = child.shape
    block = 8
    return pl.pallas_call(
        child_sum_kernel,
        out_shape=jax.ShapeDtypeStruct((tiles, pieces * tile), F32),
        grid=(devices // block,),
        in_specs=[
            pl.BlockSpec((1, 1, block * stored), lambda g: (g, 0, 0)),
            pl.BlockSpec((block, pieces, stored, tile), lambda g: (g, 0, 0, 0)),
        ],
        out_specs=pl.BlockSpec((tiles, pieces * tile), lambda g: (0, 0)),
        compiler_params=pltpu.CompilerParams(vmem_limit_bytes=24 << 20),
        cost_estimate=pl.CostEstimate(
            flops=2 * tiles * child.size,
            bytes_accessed=2 * child.size + 4 * pieces * tiles * tile,
            transcendentals=0,
        ),
        name="child_sum",
    )(target.reshape(devices // block, 1, block * stored), child)


def whole_call(kernel, name, out_shape, args, scratch=(), scalars=0, limit=32, flops=0):
    whole = pl.BlockSpec(memory_space=pltpu.VMEM)
    moved = sum(x.size * x.dtype.itemsize for x in [*args, *out_shape])
    return pl.pallas_call(
        kernel,
        out_shape=out_shape,
        in_specs=[pl.BlockSpec(memory_space=pltpu.SMEM)] * scalars
        + [whole] * (len(args) - scalars),
        out_specs=[whole] * len(out_shape),
        scratch_shapes=scratch,
        compiler_params=pltpu.CompilerParams(vmem_limit_bytes=limit << 20),
        cost_estimate=pl.CostEstimate(flops=flops, bytes_accessed=moved, transcendentals=0),
        name=name,
    )(*args)


def encode_kernel(panels, rows, deep, sums_ref, base_ref, out_ref, x_ref):
    devices, wide, tile = base_ref.shape
    cols = devices // rows
    slots = sums_ref.shape[0] // devices
    lrows = wide // deep
    lanes = 128
    each = tile // lanes
    groups = panels * each
    coded = (groups + 1) * lanes
    lane = lax.broadcasted_iota(jnp.int32, (wide, lanes), 1)
    for r in range(rows):
        powers = jnp.zeros((wide, lanes), F32)
        for k in range(panels):
            first = (r * cols + k) * slots
            child = [
                sums_ref[first : first + lrows, e * tile : (e + 1) * tile] for e in range(deep)
            ]
            x = base_ref[r * cols + k] + jnp.concatenate(child, axis=0)
            top = jnp.maximum(jnp.max(jnp.abs(x), axis=1, keepdims=True), 1e-30)
            power = jnp.floor(jnp.log(top) * 1.4426950408889634) + 1.0
            code = jnp.round(x * jnp.exp2(15.0 - power))
            code = jnp.clip(code, -32767.0, 32767.0)
            powers = jnp.where(lane == k, power, powers)
            for h in range(each):
                x_ref[k * each + h] = code[:, h * lanes : (h + 1) * lanes]
        x_ref[groups] = powers
        for g in range(groups + 1):
            across = [slice(n * coded + g * lanes, n * coded + (g + 1) * lanes) for n in range(deep + 1)]
            for e in range(deep):
                piece = x_ref[g, e * lrows : (e + 1) * lrows, :]
                piece = piece.astype(jnp.int32).astype(jnp.int16)
                for c in range(cols):
                    out_ref[r * cols + c, :, across[e]] = piece
            for u in range(cols // rows):
                some = x_ref[g, pl.ds(u, lrows, stride=wide // lrows), :]
                some = some.astype(jnp.int32).astype(jnp.int16)
                for m in range(rows):
                    out_ref[m * cols + u * rows + r, :, across[deep]] = some


def spread_rows(raw_ref, first, out_ref, source, step, count, target, tile):
    lanes = 128
    each = tile // lanes
    groups = out_ref.shape[0]
    scale = jnp.exp2(raw_ref[first + groups, pl.ds(source, count, stride=step), :] - 15.0)
    for g in range(groups):
        k = g // each
        x = raw_ref[first + g, pl.ds(source, count, stride=step), :] * scale[:, k : k + 1]
        out_ref[g, pl.ds(target, count, stride=2), :] = x


def widen(code_ref, first, raw_ref):
    lanes = 128
    for g in range(raw_ref.shape[0]):
        across = slice(first + g * lanes, first + (g + 1) * lanes)
        raw_ref[g] = code_ref[:, :, across].astype(jnp.int32).astype(F32).reshape(raw_ref.shape[1:])


def column_kernel(
    tile, panels, code_ref, wh_ref, wl_ref, gh_ref, gl_ref, raw_ref, nat_ref, xh_ref, xl_ref, acc_ref
):
    at = functools.partial(tile_at, tile)
    devices, pieces, wide = code_ref.shape
    lcols = xh_ref.shape[1] // tile
    each = tile // 128
    widen(code_ref, wide - raw_ref.shape[0] * 128, raw_ref)
    for e in range(pieces // lcols):
        for j in range(lcols):
            spread_rows(raw_ref, 0, nat_ref, e * lcols + j, pieces, devices, j * tile + e, tile)
    for k in range(panels):
        x = jnp.concatenate([nat_ref[k * each + h] for h in range(each)], axis=1)
        xh_ref[k], xl_ref[k] = split(x)

    @pl.loop(0, panels)
    def _(step):
        k = panels - 1 - step
        acc_ref[...] = jnp.zeros_like(acc_ref)

        @pl.loop(0, k + 1)
        def _(j):
            acc_ref[...] += three(
                xh_ref[j], xl_ref[j], wh_ref[at(k), at(j)], wl_ref[at(k), at(j)], NT
            )

        xh_ref[k], xl_ref[k] = split(acc_ref[...])

    @pl.loop(0, panels)
    def _(j):
        acc_ref[...] = jnp.zeros_like(acc_ref)

        @pl.loop(j, panels)
        def _(k):
            acc_ref[...] += three(
                xh_ref[k], xl_ref[k], wh_ref[at(k), at(j)], wl_ref[at(k), at(j)], NN
            )

        gh_ref[:, at(j)], gl_ref[:, at(j)] = split(acc_ref[...])


def final_kernel(
    tile,
    panels,
    where_ref,
    code_ref,
    gh_ref,
    gl_ref,
    wh_ref,
    wl_ref,
    top_ref,
    sums_ref,
    front_ref,
    out_ref,
    raw_ref,
    nat_ref,
    bh_ref,
    bl_ref,
    sum_ref,
    add_ref,
):
    lanes = 128
    each = tile // lanes
    devices, pieces, _ = code_ref.shape
    lrows = out_ref.shape[0] // tile
    lcols = out_ref.shape[1] // tile
    groups = nat_ref.shape[0]
    deep = raw_ref.shape[0] // (groups + 1)
    my_row = where_ref[0]
    my_col = where_ref[1]
    row_count = where_ref[2]
    factored = my_col < panels
    widen(code_ref, 0, raw_ref)
    for g in range(deep * each):
        sum_ref[g] = sums_ref[:, :, g * lanes : (g + 1) * lanes].reshape(sum_ref.shape[1:])
    bh_ref[...] = gh_ref[...]
    bl_ref[...] = gl_ref[...]

    @pl.when(factored)
    def _():
        bh_ref[:tile] = wh_ref[...]
        bl_ref[:tile] = wl_ref[...]

    @pl.loop(0, lrows)
    def _(i):
        rows = tile_at(tile, i)
        for e in range(deep):
            spread_rows(raw_ref, e * (groups + 1), nat_ref, i, pieces, devices, e, tile)
            for j in range(lcols):
                for h in range(each):
                    add_ref[j * each + h, pl.ds(e, devices, stride=2), :] = sum_ref[
                        e * each + h, pl.ds(j * lrows + i, devices, stride=lcols * lrows), :
                    ]
        x = jnp.concatenate([nat_ref[g] for g in range(nat_ref.shape[0])], axis=1)
        ah, al = split(x)
        leading = my_row + row_count * i < panels
        for j in range(lcols):
            here = slice(j * tile, (j + 1) * tile)
            product = three(ah, al, bh_ref[here], bl_ref[here], NT)
            child = jnp.concatenate([add_ref[j * each + h] for h in range(each)], axis=1)
            value = front_ref[rows, here] + child - product
            cleared = jnp.zeros_like(value)
            if j == 0:
                value = jnp.where(factored, product, value)
                cleared = jnp.where(factored, top_ref[...], cleared)
            out_ref[rows, here] = jnp.where(leading, cleared, value)


def shards(parent_front, child_tiles, tile_target):
    lrows = parent_front.shape[0]
    tile = parent_front.shape[2]
    lcols = parent_front.shape[3]
    row_count = lax.axis_size("row")
    col_count = lax.axis_size("col")
    devices = row_count * col_count
    order = PANELS * tile
    half = order // 2
    part = tile // col_count
    deep = tile // devices
    slots = lrows * lcols
    lanes = 128
    groups = order // lanes
    my_row = lax.axis_index("row")
    my_col = lax.axis_index("col")
    where = jnp.stack([my_row, my_col, jnp.int32(row_count)]).astype(jnp.int32)
    stored = child_tiles.shape[1]
    shape = jax.ShapeDtypeStruct

    cut = cut_rows(child_tiles.reshape(stored, tile, tile), devices)

    mine = parent_front[0, 0, :, 0, 0, :].reshape(col_count, part, tile)
    mine = lax.all_to_all(mine, "col", 0, 0, tiled=True)
    mine, cut = lax.optimization_barrier((mine, cut))
    mine = mine[:PANELS].transpose(1, 0, 2).reshape(part, order)
    moved = lax.ppermute(mine[:, half:], "row", [(5, 6), (4, 7), (3, 0)])
    first = jnp.concatenate([mine[:, :tile], moved[:, : half - tile]], axis=1)
    packed = jnp.where(my_row >= PANELS, moved, jnp.where(my_row == 0, first, mine[:, :half]))
    places = {(i, j): (i, j) for i in range(PANELS) for j in range(min(i, 2) + 1)}
    places |= {(3, 3): (0, 1), (4, 3): (7, 0), (4, 4): (7, 1)}
    places |= {(5, 3): (6, 0), (5, 4): (6, 1), (5, 5): (6, 2)}
    cut, packed = lax.optimization_barrier((cut, packed))
    packed = lax.all_gather(packed, BOTH, axis=0, tiled=True)
    spread = lax.all_to_all(cut, BOTH, split_axis=0, concat_axis=0, tiled=True)

    later, _ = lax.optimization_barrier((parent_front, cut))
    base = later[:, 0, :, 0, 0, :].reshape(lrows, devices, deep, tile).transpose(1, 2, 0, 3)
    base = base.reshape(devices, deep * lrows, tile)
    front = later.reshape(lrows * tile, lcols * tile)
    spread, base, front = lax.optimization_barrier((spread, base, front))
    base = lax.all_to_all(base, BOTH, split_axis=0, concat_axis=0, tiled=True)

    rows_all = tile_target[:, :, 0].reshape(-1)
    cols_all = tile_target[:, :, 1].reshape(-1)
    owner = rows_all % row_count * col_count + cols_all % col_count
    target = owner * slots + cols_all // col_count * lrows + rows_all // row_count
    sums = child_sum(target, spread, devices * slots)

    (to_both,) = whole_call(
        functools.partial(encode_kernel, PANELS, row_count, deep),
        "encode",
        [shape((devices, lrows, (deep + 1) * (order + lanes)), jnp.int16)],
        [sums, base],
        scratch=[pltpu.VMEM((groups + 1, deep * lrows, lanes), F32)],
    )
    to_owner = sums.reshape(devices, slots, deep * tile).astype(F16)
    packed, _ = lax.optimization_barrier((packed, to_both))
    both = lax.all_to_all(to_both, BOTH, split_axis=0, concat_axis=0, tiled=True)
    *inverse, own_high, own_low, top = whole_call(
        functools.partial(leading_kernel, tile, PANELS, places),
        "leading",
        [shape((order, order), BF16)] * 2
        + [shape((tile, order), BF16)] * 2
        + [shape((tile, tile), F32)],
        [where, packed],
        scratch=[
            pltpu.VMEM((order, order), F32),
            pltpu.VMEM((order, order), F32),
            pltpu.VMEM((order, tile), F32),
            pltpu.VMEM((tile, tile), F32),
        ],
        scalars=1,
        limit=46,
        flops=24 * order**3,
    )
    to_owner, both, inverse = lax.optimization_barrier((to_owner, both, inverse))
    summed = lax.all_to_all(to_owner, BOTH, split_axis=0, concat_axis=0, tiled=True)

    right = whole_call(
        functools.partial(column_kernel, tile, PANELS),
        "column",
        [shape((lcols * tile, order), BF16)] * 2,
        [both, *inverse],
        scratch=[
            pltpu.VMEM((groups + 1, lcols * tile, lanes), F32),
            pltpu.VMEM((groups, lcols * tile, lanes), F32),
            pltpu.VMEM((PANELS, lcols * tile, tile), BF16),
            pltpu.VMEM((PANELS, lcols * tile, tile), BF16),
            pltpu.VMEM((lcols * tile, tile), F32),
        ],
        limit=36,
        flops=12 * lcols * tile * order**2,
    )
    (result,) = whole_call(
        functools.partial(final_kernel, tile, PANELS),
        "final",
        [shape(front.shape, F32)],
        [where, both, *right, own_high, own_low, top, summed.astype(F32), front],
        scratch=[
            pltpu.VMEM((deep * (groups + 1), devices * lrows, lanes), F32),
            pltpu.VMEM((groups, tile, lanes), F32),
            pltpu.VMEM((lcols * tile, order), BF16),
            pltpu.VMEM((lcols * tile, order), BF16),
            pltpu.VMEM((deep * tile // lanes, devices * slots, lanes), F32),
            pltpu.VMEM((lcols * tile // lanes, tile, lanes), F32),
        ],
        scalars=1,
        limit=40,
        flops=6 * lrows * tile * lcols * tile * order,
    )
    return result.reshape(parent_front.shape)


def solution(mesh):
    return jax.shard_map(
        shards,
        mesh=mesh,
        in_specs=(
            P(None, "row", None, None, "col", None),
            P(("row", "col"), None, None, None),
            P(),
        ),
        out_specs=P(None, "row", None, None, "col", None),
        check_vma=False,
    )
```

time: 376 us -> 324 us (0.86)
  waiting for transfers between devices: 132 us -> 92.9 us
  local copies, waits for them, and re-layouts: 56.9 us -> 27.7 us
  starting transfers between devices: 38.9 us -> 49.6 us
  Pallas kernels: 121 us -> 127 us
    pallas_call x4, Pallas kernels: 31 us -> 97.1 us  [whole_call(): pl.pallas_call(kernel, out_shape=out_shape, in_specs=[pl.BlockSpec(memory...]
    pallas_call x2 -> x0, Pallas kernels: 62.1 us -> none  [the longest x1 42.2 us: factor_leading(): pl.pallas_call(functools.partial(factor_kernel, tile, panels), out_shape=...]
    all_to_all x2, waiting for transfers between devices: 15.9 us -> 0.01 us  [the longest x1 0.01 us: shards(): lax.all_to_all(to_both, BOTH, split_axis=0, concat_axis=0, tiled=True)]
    unnamed x41 -> x29, local copies, waits for them, and re-layouts: 35 us -> 19.1 us
    all_to_all x1, waiting for transfers between devices: 100 us -> 87.7 us  [shards(): spread = lax.all_to_all(cut, BOTH, split_axis=0, concat_axis=0, tiled=True)]
    unnamed x1 -> x0, other arithmetic: 9.02 us -> none
    all_to_all x1, starting transfers between devices: 6.3 us -> 15.3 us  [shards(): spread = lax.all_to_all(cut, BOTH, split_axis=0, concat_axis=0, tiled=True)]
    all_gather x1, waiting for transfers between devices: 11.1 us -> 2.95 us  [shards(): packed = lax.all_gather(packed, BOTH, axis=0, tiled=True)]
  transfers between devices with their start and end apart: 6 -> 7, of which waited for: 4 -> 3; matrix products, arithmetic and copies ran while one was open for 1% -> 4% of each run, Pallas kernels for 30% -> 36%
where the time goes in v1:
time: 324 us; the launch traced here: 323 us
  Pallas kernels  127 us (39%)
  waiting for transfers between devices  92.9 us (29%)
  starting transfers between devices  49.6 us (15%)
  local copies, waits for them, and re-layouts  27.7 us (9%)
  between operations  13.6 us (4%)
  other arithmetic  11.8 us (4%)
    pallas_call x4, Pallas kernels, whole_call(): pl.pallas_call(kernel, out_shape=out_shape, in_specs=[pl.BlockSpec(memory...  97.1 us
    all_to_all x1, waiting for transfers between devices, shards(): spread = lax.all_to_all(cut, BOTH, split_axis=0, concat_axis=0, tiled=True)  87.7 us
    unnamed x29, local copies, waits for them, and re-layouts  19.1 us
    all_to_all x1, starting transfers between devices, shards(): spread = lax.all_to_all(cut, BOTH, split_axis=0, concat_axis=0, tiled=True)  15.3 us
    pallas_call x1, Pallas kernels, child_sum(): pl.pallas_call(child_sum_kernel, out_shape=jax.ShapeDtypeStruct((tiles, p...  15.2 us
    pallas_call x1, Pallas kernels, cut_rows(): pl.pallas_call(cut_kernel, out_shape=jax.ShapeDtypeStruct((devices, deep,...  14.8 us
    all_to_all x1, starting transfers between devices, shards(): base = lax.all_to_all(base, BOTH, split_axis=0, concat_axis=0, tiled=True)  9.96 us
    all_to_all x1, starting transfers between devices, shards(): mine = lax.all_to_all(mine, 'col', 0, 0, tiled=True)  8.43 us
  transfers between devices with their start and end apart: 7, of which 3 were waited for; matrix products, arithmetic and copies ran while one was open for 4% of the time, Pallas kernels for 36%

profile of v1, /device:TPU:1, one launch (start us, length us, event | category | flops | bytes accessed | tf_op | source)
XLA Modules:
  0.0 322.7 jit_solution(9799093857111073164)
XLA Ops:
  6.5 1.1 slice.29
  7.7 0.7 copy.36
  8.4 8.4 %all-to-all-start = ((f32[16,16,256]{2,1,0:T(8,128)}), f32[16,16,256]{2,1,0:T(8,128)S(1)}, u32[]{:S(2)}, u32[]{:S(2)}) async-start(f32[16,16,256]{2,1,0:T(8,128)} %bitcast.8), calls=%async_computation | async-start | bytes 524288 | tf_op jit(solution)/shard_map/all_to_all | solution.py:421
  16.8 0.0 all-gather.2.cloned.1.call-start
  16.9 14.8 %cut_rows.1 = bf16[128,2,64,256]{3,2,1,0:T(8,128)(2,1)} custom-call(bf16[64,256,256]{2,1,0:T(8,128)(2,1)} %bitcast.21), custom_call_target="tpu_custom_call" | custom-call | flops 4194304 | bytes 16777216 | tf_op jit(solution)/shard_map/cut_rows/pallas_call | solution.py:165
  31.7 0.7 collective-permute-start
  32.4 0.6 fusion
  33.1 0.0 all-gather.2.cloned.1.call-update
  33.1 15.3 %all-to-all-start.1 = ((bf16[128,2,64,256]{3,2,1,0:T(8,128)(2,1)}), bf16[128,2,64,256]{3,2,1,0:T(8,128)(2,1)}, u32[]{:S(2)}, u32[]{:S(2)}) async-start(bf16[128,2,64,256]{3,2,1,0:T(8,128)(2,1)} %cut_rows.1), calls=%async_computation.1 | async-start | bytes 16777216 | tf_op jit(solution)/shard_map/all_to_all | solution.py:432
  48.4 0.0 slice-start
  48.4 0.1 fusion.3
  48.5 0.1 copy.22
  48.6 0.1 reshape_squeeze.16
  48.7 0.1 copy.26
  48.8 0.1 reshape_squeeze.17
  48.9 0.1 pad_add_fusion.where_ref
  49.0 0.5 add_add_fusion.target_ref
  49.5 0.2 slice-done
  49.6 0.7 copy.35
  50.3 1.4 reshape.228
  51.7 7.7 %reduce = f32[4,256,2,256]{3,2,1,0:T(2,128)S(1)} reduce(f32[4,1,256,2,1,256]{5,4,3,2,1,0:T(1,128)} %param.3, f32[]{:T(128)} %constant.67), dimensions={1,4}, to_apply=%get-tuple-element.28.reduce_sub_computation | reduce | bytes 4194308 | tf_op jit(solution)/shard_map/optimization_barrier | solution.py:434
  59.4 1.5 copy.38
  60.9 87.7 %all-to-all-done.1.child_ref = bf16[128,2,64,256]{3,2,1,0:T(8,128)(2,1)} async-done(((bf16[128,2,64,256]{3,2,1,0:T(8,128)(2,1)}), bf16[128,2,64,256]{3,2,1,0:T(8,128)(2,1)}, u32[]{:S(2)}, u32[]{:S(2)}) %all-to-all-start.1) | async-done | bytes 8388640 | tf_op jit(solution)/shard_map/all_to_all | solution.py:432
  148.6 10.0 %all-to-all-start.2 = ((f32[128,8,256]{2,1,0:T(8,128)}), f32[128,8,256]{2,1,0:T(8,128)S(1)}, u32[]{:S(2)}, u32[]{:S(2)}) async-start(f32[128,8,256]{2,1,0:T(8,128)} %reshape.228), calls=%async_computation.2 | async-start | bytes 2097152 | tf_op jit(solution)/shard_map/all_to_all | solution.py:439
  158.6 15.2 %child_sum.1.sums_ref = f32[1024,512]{1,0:T(8,128)S(1)} custom-call(s32[16,1,512]{2,1,0:T(1,128)S(1)} %add_add_fusion.target_ref, bf16[128,2,64,256]{3,2,1,0:T(8,128)(2,1)} %all-to-all-done.1.child_ref), custom_call_target="tpu_custom_call" | custom-call | flops 8589934592 | bytes 10485760 | tf_op jit(solution)/shard_map/child_sum/pallas_call | solution.py:197
  173.8 1.2 convert_bitcast_fusion
  175.0 2.2 all-to-all-done.2.base_ref
  177.2 1.6 encode.1
  178.9 2.3 copy-done
  181.2 8.0 %all-to-all-start.3 = ((s16[128,4,4992]{2,1,0:T(4,128)(2,1)}), s16[128,4,4992]{2,1,0:T(4,128)(2,1)}, u32[]{:S(2)}, u32[]{:S(2)}) async-start(s16[128,4,4992]{2,1,0:T(4,128)(2,1)} %copy-done), calls=%async_computation.3 | async-start | bytes 10223616 | tf_op jit(solution)/shard_map/all_to_all | solution.py:456
  189.1 2.9 all-gather.2.cloned.1.call-done.a_ref
  192.1 63.3 %leading.1 = (bf16[1536,1536]{1,0:T(8,128)(2,1)S(1)}, bf16[1536,1536]{1,0:T(8,128)(2,1)}, bf16[256,1536]{1,0:T(8,128)(2,1)S(1)}, bf16[256,1536]{1,0:T(8,128)(2,1)S(1)}, f32[256,256]{1,0:T(8,128)S(1)}) custom-call(s32[3]{0:T(128)S(1)} %pad_add_fusion.where_ref, f32[2048,768]{1,0:T(8,128)} %all-gather.2.cloned.1.call-done.a_ref), custom_call_target="tpu_custom_call" | custom-call | flops 86973087744 | bytes 17563660 | tf_op jit(solution)/shard_map/leading/pallas_call | solution.py:219
  255.4 0.9 copy-done.7
  256.3 2.1 copy-done.9
  258.4 7.3 %all-to-all-start.4 = ((f16[128,8,512]{2,1,0:T(8,128)(2,1)}), f16[128,8,512]{2,1,0:T(8,128)(2,1)}, u32[]{:S(2)}, u32[]{:S(2)}) async-start(f16[128,8,512]{2,1,0:T(8,128)(2,1)} %convert_bitcast_fusion), calls=%async_computation.4 | async-start | bytes 2097152 | tf_op jit(solution)/shard_map/all_to_all | solution.py:475
  265.8 2.3 copy-done.10
  268.1 2.3 copy-done.11
  270.4 21.5 %column.1 = (bf16[512,1536]{1,0:T(8,128)(2,1)S(1)}, bf16[512,1536]{1,0:T(8,128)(2,1)S(1)}) custom-call(s16[128,4,4992]{2,1,0:T(4,128)(2,1)} %all-to-all-done.3.code_ref, bf16[1536,1536]{1,0:T(8,128)(2,1)S(1)} %copy-done.10, bf16[1536,1536]{1,0:T(8,128)(2,1)S(1)} %copy-done.11), custom_call_target="tpu_custom_call" | custom-call | flops 14495514624 | bytes 17694720 | tf_op jit(solution)/shard_map/column/pallas_call | solution.py:219
  292.0 1.1 copy-done.3
  293.1 1.2 copy-done.5
  294.3 1.7 convert_element_type.11.sums_ref
  296.0 0.2 copy-done.1
  296.2 0.2 copy-done.8
  296.4 1.4 copy-done.4
  297.8 1.4 copy-done.6
  299.2 10.6 %final.1 = f32[1024,512]{1,0:T(8,128)S(1)} custom-call(s32[3]{0:T(128)S(1)} %pad_add_fusion.where_ref, s16[128,4,4992]{2,1,0:T(4,128)(2,1)} %all-to-all-done.3.code_ref, bf16[512,1536]{1,0:T(8,128)(2,1)S(1)} %copy-done.4, bf16[512,1536]{1,0:T(8,128)(2,1)S(1)} %copy-done.6, bf16[256,1536]{1,0:T(8,128)(2,1)S(1)} %get-tuple-element.40.wh_ref, ...), custom_call_target="tpu_custom_call" | custom-call | flops 4831838208 | bytes 16384012 | tf_op jit(solution)/shard_map/final/pallas_call | solution.py:219
  309.8 1.3 copy-done.2
  311.2 4.7 %reshape.231 = f32[4,1,256,2,1,256]{5,4,3,2,1,0:T(1,128)} reshape(f32[1024,512]{1,0:T(8,128)} %copy-done.2) | data formatting | bytes 4194304 | tf_op jit(solution)/shard_map/reshape | solution.py:509
  (23 shorter events, 0.1 us)
Async XLA Ops:
  8.4 23.3 %all-to-all-start = ((f32[16,16,256]{2,1,0:T(8,128)}), f32[16,16,256]{2,1,0:T(8,128)S(1)}, u32[]{:S(2)}, u32[]{:S(2)}) async-start(f32[16,16,256]{2,1,0:T(8,128)} %bitcast.8), calls=%async_computation | async-start | bytes 524288 | tf_op jit(solution)/shard_map/all_to_all | solution.py:421
  16.8 175.3 %all-gather.2.cloned.1.call-start = ((), (), s32[]{:S(2)}) async-start(), calls=%async_computation.5 | async-start | bytes 6340608 | tf_op jit(solution)/shard_map/all_gather | solution.py:431
  31.7 0.7 collective-permute-start
  33.1 15.3 %copy-start.12 = (s32[128,64,2]{0,2,1:T(2,128)S(1)}, s32[128,64,2]{0,2,1:T(2,128)}, u32[]{:S(2)}) copy-start(s32[128,64,2]{0,2,1:T(2,128)} %param.5) | copy-start | bytes 196612
  33.1 115.5 %all-to-all-start.1 = ((bf16[128,2,64,256]{3,2,1,0:T(8,128)(2,1)}), bf16[128,2,64,256]{3,2,1,0:T(8,128)(2,1)}, u32[]{:S(2)}, u32[]{:S(2)}) async-start(bf16[128,2,64,256]{3,2,1,0:T(8,128)(2,1)} %cut_rows.1), calls=%async_computation.1 | async-start | bytes 16777216 | tf_op jit(solution)/shard_map/all_to_all | solution.py:432
  48.4 1.2 slice-start
  148.6 28.6 %all-to-all-start.2 = ((f32[128,8,256]{2,1,0:T(8,128)}), f32[128,8,256]{2,1,0:T(8,128)S(1)}, u32[]{:S(2)}, u32[]{:S(2)}) async-start(f32[128,8,256]{2,1,0:T(8,128)} %reshape.228), calls=%async_computation.2 | async-start | bytes 2097152 | tf_op jit(solution)/shard_map/all_to_all | solution.py:439
  178.9 2.3 copy-start
  181.2 77.3 %all-to-all-start.3 = ((s16[128,4,4992]{2,1,0:T(4,128)(2,1)}), s16[128,4,4992]{2,1,0:T(4,128)(2,1)}, u32[]{:S(2)}, u32[]{:S(2)}) async-start(s16[128,4,4992]{2,1,0:T(4,128)(2,1)} %copy-done), calls=%async_computation.3 | async-start | bytes 10223616 | tf_op jit(solution)/shard_map/all_to_all | solution.py:456
  255.4 0.9 copy-start.7
  256.3 2.1 copy-start.9
  258.4 35.9 %all-to-all-start.4 = ((f16[128,8,512]{2,1,0:T(8,128)(2,1)}), f16[128,8,512]{2,1,0:T(8,128)(2,1)}, u32[]{:S(2)}, u32[]{:S(2)}) async-start(f16[128,8,512]{2,1,0:T(8,128)(2,1)} %convert_bitcast_fusion), calls=%async_computation.4 | async-start | bytes 2097152 | tf_op jit(solution)/shard_map/all_to_all | solution.py:475
  265.7 2.3 copy-start.10
  268.1 2.3 copy-start.11
  292.0 1.2 copy-start.3
  293.1 1.2 copy-start.5
  294.3 1.9 copy-start.1
  294.3 2.1 copy-start.8
  296.4 1.4 copy-start.4
  297.8 1.4 copy-start.6
  309.8 1.3 copy-start.2
Sparse Core Ops, SparseCore 0:
  33.2 158.8 all-gather.1

commit v2 on v1

--- a/solution.py
+++ b/solution.py
@@ -58,6 +58,8 @@
     own_low_ref,
     top_ref,
     l_ref,
+    lh_ref,
+    ll_ref,
     s_ref,
     d_ref,
     acc_ref,
@@ -82,12 +84,9 @@
         only = jnp.where(diag, block, 0.0)
         down = lax.rsqrt(jnp.sum(only, axis=1, keepdims=True))
         across = lax.rsqrt(jnp.sum(only, axis=0, keepdims=True))
-        d_ref[here, :] = jnp.where(diag, down, 0.0)
-        acc_ref[...] = block * down * across - eye
-
-        def improve():
-            w = d_ref[here, :]
-            d_ref[here, :] = w - dot(acc_ref[...] * weight, w, NN)
+        first = block * down * across - eye
+
+        d_ref[here, :] = (eye - first * weight) * across
 
         def unfinished(state):
             step, worst = state
@@ -95,34 +94,40 @@
 
         def refine(state):
             step, _ = state
-            improve()
             w = d_ref[here, :]
             left = dot(dot(w, s_ref[here, here], NN), w, NT) - eye
-            acc_ref[...] = left
+            d_ref[here, :] = w - dot3(left * weight, w, NN)
             return step + 1, jnp.max(jnp.abs(left))
 
-        lax.while_loop(unfinished, refine, (jnp.int32(0), jnp.max(jnp.abs(acc_ref[...]))))
-        improve()
-        l_ref[here, here] = jnp.where(
-            rows >= cols, dot(s_ref[here, here], d_ref[here, :], NT), 0.0
-        )
+        lax.while_loop(unfinished, refine, (jnp.int32(0), jnp.float32(1.0)))
+        dh, dl = split(d_ref[here, :])
+        lower = three(*split(s_ref[here, here]), dh, dl, NT)
+        l_ref[here, here] = jnp.where(rows >= cols, lower, 0.0)
 
         @pl.loop(k + 1, panels)
         def _(i):
-            l_ref[at(i), here] = dot3(s_ref[at(i), here], d_ref[here, :], NT)
+            below = three(*split(s_ref[at(i), here]), *split(d_ref[here, :]), NT)
+            l_ref[at(i), here] = below
+            lh_ref[at(i), here], ll_ref[at(i), here] = split(below)
 
         @pl.loop(k + 1, panels)
         def _(i):
             @pl.loop(k + 1, i + 1)
             def _(j):
-                s_ref[at(i), at(j)] -= dot3(l_ref[at(i), here], l_ref[at(j), here], NT)
-
-    w_ref = s_ref
-    w_ref[...] = jnp.zeros_like(w_ref)
+                s_ref[at(i), at(j)] -= three(
+                    lh_ref[at(i), here],
+                    ll_ref[at(i), here],
+                    lh_ref[at(j), here],
+                    ll_ref[at(j), here],
+                    NT,
+                )
+
+    high_ref[...] = jnp.zeros_like(high_ref)
+    low_ref[...] = jnp.zeros_like(low_ref)
 
     @pl.loop(0, panels)
     def _(i):
-        w_ref[at(i), at(i)] = d_ref[at(i), :]
+        high_ref[at(i), at(i)], low_ref[at(i), at(i)] = split(d_ref[at(i), :])
 
     @pl.loop(1, panels)
     def _(i):
@@ -132,17 +137,23 @@
 
             @pl.loop(j, i)
             def _(m):
-                acc_ref[...] += dot3(l_ref[at(i), at(m)], w_ref[at(m), at(j)], NN)
-
-            w_ref[at(i), at(j)] = -dot3(d_ref[at(i), :], acc_ref[...], NN)
-
-    @pl.loop(0, panels)
-    def _(i):
-        high_ref[at(i), :], low_ref[at(i), :] = split(w_ref[at(i), :])
+                acc_ref[...] += three(
+                    lh_ref[at(i), at(m)],
+                    ll_ref[at(i), at(m)],
+                    high_ref[at(m), at(j)],
+                    low_ref[at(m), at(j)],
+                    NN,
+                )
+
+            entry = -three(
+                high_ref[at(i), at(i)], low_ref[at(i), at(i)], *split(acc_ref[...]), NN
+            )
+            high_ref[at(i), at(j)], low_ref[at(i), at(j)] = split(entry)
 
     r = jnp.minimum(where_ref[0], panels - 1)
     c = jnp.minimum(where_ref[1], panels - 1)
-    own_high_ref[...], own_low_ref[...] = split(w_ref[at(c), :])
+    own_high_ref[...] = high_ref[at(c), :]
+    own_low_ref[...] = low_ref[at(c), :]
     top_ref[...] = l_ref[at(r), at(c)]
 
 
@@ -158,29 +169,30 @@
                 out_ref[d, e, :, across] = rows.astype(BF16)
 
 
-def cut_rows(child, devices):
+def cut_rows(child, devices, share, shares):
     stored, tile, _ = child.shape
+    stored = stored // shares
     deep = tile // devices
     block = 8
     return pl.pallas_call(
         cut_kernel,
         out_shape=jax.ShapeDtypeStruct((devices, deep, stored, tile), BF16),
         grid=(devices // block,),
-        in_specs=[pl.BlockSpec((stored, block * deep, tile), lambda g: (0, g, 0))],
+        in_specs=[pl.BlockSpec((stored, block * deep, tile), lambda g: (share, g, 0))],
         out_specs=pl.BlockSpec((block, deep, stored, tile), lambda g: (g, 0, 0, 0)),
         scratch_shapes=[pltpu.VMEM((tile // 128, stored * block * deep, 128), F32)],
         compiler_params=pltpu.CompilerParams(vmem_limit_bytes=58 << 20),
         cost_estimate=pl.CostEstimate(
-            flops=child.size, bytes_accessed=4 * child.size, transcendentals=0
+            flops=child.size // shares, bytes_accessed=4 * child.size // shares, transcendentals=0
         ),
         name="cut_rows",
     )(child)
 
 
-def child_sum_kernel(target_ref, child_ref, out_ref):
+def child_sum_kernel(target_ref, child_ref, start_ref, out_ref):
     @pl.when(pl.program_id(0) == 0)
     def _():
-        out_ref[...] = jnp.zeros_like(out_ref)
+        out_ref[...] = start_ref[...]
 
     sources, pieces, stored, tile = child_ref.shape
     count = sources * stored
@@ -191,9 +203,11 @@
         out_ref[:, e * tile : (e + 1) * tile] += jnp.dot(hot, right, preferred_element_type=F32)
 
 
-def child_sum(target, child, tiles):
+def child_sum(target, child, start):
     devices, pieces, stored, tile = child.shape
-    block = 8
+    tiles = start.shape[0]
+    block = 512 // stored
+    resident = pl.BlockSpec((tiles, pieces * tile), lambda g: (0, 0))
     return pl.pallas_call(
         child_sum_kernel,
         out_shape=jax.ShapeDtypeStruct((tiles, pieces * tile), F32),
@@ -201,19 +215,20 @@
         in_specs=[
             pl.BlockSpec((1, 1, block * stored), lambda g: (g, 0, 0)),
             pl.BlockSpec((block, pieces, stored, tile), lambda g: (g, 0, 0, 0)),
+            resident,
         ],
-        out_specs=pl.BlockSpec((tiles, pieces * tile), lambda g: (0, 0)),
+        out_specs=resident,
         compiler_params=pltpu.CompilerParams(vmem_limit_bytes=24 << 20),
         cost_estimate=pl.CostEstimate(
             flops=2 * tiles * child.size,
-            bytes_accessed=2 * child.size + 4 * pieces * tiles * tile,
+            bytes_accessed=2 * child.size + 8 * pieces * tiles * tile,
             transcendentals=0,
         ),
         name="child_sum",
-    )(target.reshape(devices // block, 1, block * stored), child)
-
-
-def whole_call(kernel, name, out_shape, args, scratch=(), scalars=0, limit=32, flops=0):
+    )(target.reshape(devices // block, 1, block * stored), child, start)
+
+
+def whole_call(kernel, name, out_shape, args, scratch=(), scalars=0, limit=58, flops=0):
     whole = pl.BlockSpec(memory_space=pltpu.VMEM)
     moved = sum(x.size * x.dtype.itemsize for x in [*args, *out_shape])
     return pl.pallas_call(
@@ -351,8 +366,8 @@
     lanes = 128
     each = tile // lanes
     devices, pieces, _ = code_ref.shape
-    lrows = out_ref.shape[0] // tile
-    lcols = out_ref.shape[1] // tile
+    lrows = front_ref.shape[0] // tile
+    lcols = front_ref.shape[1] // tile
     groups = nat_ref.shape[0]
     deep = raw_ref.shape[0] // (groups + 1)
     my_row = where_ref[0]
@@ -392,7 +407,12 @@
             if j == 0:
                 value = jnp.where(factored, product, value)
                 cleared = jnp.where(factored, top_ref[...], cleared)
-            out_ref[rows, here] = jnp.where(leading, cleared, value)
+            value = jnp.where(leading, cleared, value)
+            for h in range(each):
+                start = i * (tile * lcols * each) + j * each + h
+                out_ref[pl.ds(start, tile, stride=lcols * each), :] = value[
+                    :, h * lanes : (h + 1) * lanes
+                ]
 
 
 def shards(parent_front, child_tiles, tile_target):
@@ -415,7 +435,8 @@
     stored = child_tiles.shape[1]
     shape = jax.ShapeDtypeStruct
 
-    cut = cut_rows(child_tiles.reshape(stored, tile, tile), devices)
+    held = child_tiles.reshape(stored, tile, tile)
+    cut = cut_rows(held, devices, 0, 2)
 
     mine = parent_front[0, 0, :, 0, 0, :].reshape(col_count, part, tile)
     mine = lax.all_to_all(mine, "col", 0, 0, tiled=True)
@@ -430,19 +451,27 @@
     cut, packed = lax.optimization_barrier((cut, packed))
     packed = lax.all_gather(packed, BOTH, axis=0, tiled=True)
     spread = lax.all_to_all(cut, BOTH, split_axis=0, concat_axis=0, tiled=True)
+    held, _ = lax.optimization_barrier((held, cut))
+    cut = cut_rows(held, devices, 1, 2)
+    cut, spread = lax.optimization_barrier((cut, spread))
+    second = lax.all_to_all(cut, BOTH, split_axis=0, concat_axis=0, tiled=True)
 
     later, _ = lax.optimization_barrier((parent_front, cut))
     base = later[:, 0, :, 0, 0, :].reshape(lrows, devices, deep, tile).transpose(1, 2, 0, 3)
     base = base.reshape(devices, deep * lrows, tile)
     front = later.reshape(lrows * tile, lcols * tile)
-    spread, base, front = lax.optimization_barrier((spread, base, front))
-    base = lax.all_to_all(base, BOTH, split_axis=0, concat_axis=0, tiled=True)
+    second, base, front = lax.optimization_barrier((second, base, front))
 
     rows_all = tile_target[:, :, 0].reshape(-1)
     cols_all = tile_target[:, :, 1].reshape(-1)
     owner = rows_all % row_count * col_count + cols_all % col_count
     target = owner * slots + cols_all // col_count * lrows + rows_all // row_count
-    sums = child_sum(target, spread, devices * slots)
+    target = target.reshape(devices, stored)
+    sums = jnp.zeros((devices * slots, deep * tile), F32)
+    sums = child_sum(target[:, : stored // 2], spread, sums)
+    second, sums, base = lax.optimization_barrier((second, sums, base))
+    base = lax.all_to_all(base, BOTH, split_axis=0, concat_axis=0, tiled=True)
+    sums = child_sum(target[:, stored // 2 :], second, sums)
 
     (to_both,) = whole_call(
         functools.partial(encode_kernel, PANELS, row_count, deep),
@@ -463,15 +492,17 @@
         [where, packed],
         scratch=[
             pltpu.VMEM((order, order), F32),
+            pltpu.VMEM((order, order), BF16),
+            pltpu.VMEM((order, order), BF16),
             pltpu.VMEM((order, order), F32),
             pltpu.VMEM((order, tile), F32),
             pltpu.VMEM((tile, tile), F32),
         ],
         scalars=1,
-        limit=46,
+        limit=58,
         flops=24 * order**3,
     )
-    to_owner, both, inverse = lax.optimization_barrier((to_owner, both, inverse))
+    to_owner, both, top = lax.optimization_barrier((to_owner, both, top))
     summed = lax.all_to_all(to_owner, BOTH, split_axis=0, concat_axis=0, tiled=True)
 
     right = whole_call(
@@ -486,13 +517,13 @@
             pltpu.VMEM((PANELS, lcols * tile, tile), BF16),
             pltpu.VMEM((lcols * tile, tile), F32),
         ],
-        limit=36,
+        limit=58,
         flops=12 * lcols * tile * order**2,
     )
     (result,) = whole_call(
         functools.partial(final_kernel, tile, PANELS),
         "final",
-        [shape(front.shape, F32)],
+        [shape((front.size // lanes, lanes), F32)],
         [where, both, *right, own_high, own_low, top, summed.astype(F32), front],
         scratch=[
             pltpu.VMEM((deep * (groups + 1), devices * lrows, lanes), F32),
@@ -503,7 +534,7 @@
             pltpu.VMEM((lcols * tile // lanes, tile, lanes), F32),
         ],
         scalars=1,
-        limit=40,
+        limit=58,
         flops=6 * lrows * tile * lcols * tile * order,
     )
     return result.reshape(parent_front.shape)

time: 324 us -> 316 us (0.975)
  local copies, waits for them, and re-layouts: 27.7 us -> 10.8 us
  Pallas kernels: 127 us -> 141 us
  starting transfers between devices: 49.6 us -> 44.2 us
    all_to_all x1, waiting for transfers between devices: 87.7 us -> 41.1 us  [shards(): spread = lax.all_to_all(cut, BOTH, split_axis=0, concat_axis=0, tiled=True)]
    all_to_all x0 -> x1, waiting for transfers between devices: none -> 31.6 us  [shards(): second = lax.all_to_all(cut, BOTH, split_axis=0, concat_axis=0, tiled=True)]
    unnamed x29 -> x13, local copies, waits for them, and re-layouts: 19.1 us -> 6.09 us
    all_to_all x1, waiting for transfers between devices: 2.19 us -> 13.3 us  [shards(): base = lax.all_to_all(base, BOTH, split_axis=0, concat_axis=0, tiled=True)]
    pallas_call x1 -> x2, Pallas kernels: 14.8 us -> 23 us  [cut_rows(): pl.pallas_call(cut_kernel, out_shape=jax.ShapeDtypeStruct((devices, deep,...]
    all_to_all x1, waiting for transfers between devices: 0.01 us -> 6.8 us  [shards(): lax.all_to_all(to_both, BOTH, split_axis=0, concat_axis=0, tiled=True)]
    all_to_all x1, starting transfers between devices: 9.96 us -> 4.46 us  [shards(): base = lax.all_to_all(base, BOTH, split_axis=0, concat_axis=0, tiled=True)]
    all_to_all x0 -> x1, starting transfers between devices: none -> 5.08 us  [shards(): second = lax.all_to_all(cut, BOTH, split_axis=0, concat_axis=0, tiled=True)]
  transfers between devices with their start and end apart: 7 -> 8, of which waited for: 3 -> 4; matrix products, arithmetic and copies ran while one was open for 4% -> 4% of each run, Pallas kernels for 36% -> 40%
where the time goes in v2:
time: 316 us; the launch traced here: 314 us
  Pallas kernels  141 us (45%)
  waiting for transfers between devices  92.9 us (29%)
  starting transfers between devices  44.2 us (14%)
  between operations  13.6 us (4%)
  other arithmetic  12.1 us (4%)
  local copies, waits for them, and re-layouts  10.8 us (3%)
    pallas_call x4, Pallas kernels, whole_call(): pl.pallas_call(kernel, out_shape=out_shape, in_specs=[pl.BlockSpec(memory...  102 us
    all_to_all x1, waiting for transfers between devices, shards(): spread = lax.all_to_all(cut, BOTH, split_axis=0, concat_axis=0, tiled=True)  41.1 us
    all_to_all x1, waiting for transfers between devices, shards(): second = lax.all_to_all(cut, BOTH, split_axis=0, concat_axis=0, tiled=True)  31.6 us
    pallas_call x2, Pallas kernels, cut_rows(): pl.pallas_call(cut_kernel, out_shape=jax.ShapeDtypeStruct((devices, deep,...  23 us
    pallas_call x2, Pallas kernels, child_sum(): pl.pallas_call(child_sum_kernel, out_shape=jax.ShapeDtypeStruct((tiles, p...  16.2 us
    all_to_all x1, starting transfers between devices, shards(): spread = lax.all_to_all(cut, BOTH, split_axis=0, concat_axis=0, tiled=True)  15.3 us
    all_to_all x1, waiting for transfers between devices, shards(): base = lax.all_to_all(base, BOTH, split_axis=0, concat_axis=0, tiled=True)  13.3 us
    all_to_all x1, starting transfers between devices, shards(): mine = lax.all_to_all(mine, 'col', 0, 0, tiled=True)  8.43 us
  transfers between devices with their start and end apart: 8, of which 4 were waited for; matrix products, arithmetic and copies ran while one was open for 4% of the time, Pallas kernels for 40%

profile of v2, /device:TPU:1, one launch (start us, length us, event | category | flops | bytes accessed | tf_op | source)
XLA Modules:
  0.0 314.4 jit_solution(6846379203201886033)
XLA Ops:
  6.5 1.1 slice.36
  7.7 0.7 copy.27
  8.4 8.4 %all-to-all-start = ((f32[16,16,256]{2,1,0:T(8,128)}), f32[16,16,256]{2,1,0:T(8,128)S(1)}, u32[]{:S(2)}, u32[]{:S(2)}) async-start(f32[16,16,256]{2,1,0:T(8,128)} %bitcast.11), calls=%async_computation | async-start | bytes 524288 | tf_op jit(solution)/shard_map/all_to_all | solution.py:442
  16.8 0.0 all-gather.2.cloned.1.call-start
  16.9 11.5 %cut_rows.2 = bf16[128,2,32,256]{3,2,1,0:T(8,128)(2,1)} custom-call(bf16[64,256,256]{2,1,0:T(8,128)(2,1)} %bitcast.21), custom_call_target="tpu_custom_call" | custom-call | flops 2097152 | bytes 8388608 | tf_op jit(solution)/shard_map/cut_rows/pallas_call | solution.py:177
  28.4 0.0 all-to-all-done
  28.5 0.7 collective-permute-start
  29.1 0.0 collective-permute-done
  29.2 0.6 fusion
  29.8 0.0 all-gather.2.cloned.1.call-update
  29.8 15.3 %all-to-all-start.1 = ((bf16[128,2,32,256]{3,2,1,0:T(8,128)(2,1)}), bf16[128,2,32,256]{3,2,1,0:T(8,128)(2,1)}, u32[]{:S(2)}, u32[]{:S(2)}) async-start(bf16[128,2,32,256]{3,2,1,0:T(8,128)(2,1)} %cut_rows.2), calls=%async_computation.1 | async-start | bytes 8388608 | tf_op jit(solution)/shard_map/all_to_all | solution.py:453
  45.1 11.5 %cut_rows.3 = bf16[128,2,32,256]{3,2,1,0:T(8,128)(2,1)} custom-call(bf16[64,256,256]{2,1,0:T(8,128)(2,1)} %bitcast.22), custom_call_target="tpu_custom_call" | custom-call | flops 2097152 | bytes 8388608 | tf_op jit(solution)/shard_map/cut_rows/pallas_call | solution.py:177
  56.6 41.1 %all-to-all-done.1.child_ref = bf16[128,2,32,256]{3,2,1,0:T(8,128)(2,1)} async-done(((bf16[128,2,32,256]{3,2,1,0:T(8,128)(2,1)}), bf16[128,2,32,256]{3,2,1,0:T(8,128)(2,1)}, u32[]{:S(2)}, u32[]{:S(2)}) %all-to-all-start.1) | async-done | bytes 4194336 | tf_op jit(solution)/shard_map/all_to_all | solution.py:453
  97.7 5.1 %all-to-all-start.2 = ((bf16[128,2,32,256]{3,2,1,0:T(8,128)(2,1)}), bf16[128,2,32,256]{3,2,1,0:T(8,128)(2,1)}, u32[]{:S(2)}, u32[]{:S(2)}) async-start(bf16[128,2,32,256]{3,2,1,0:T(8,128)(2,1)} %cut_rows.3), calls=%async_computation.2 | async-start | bytes 8388608 | tf_op jit(solution)/shard_map/all_to_all | solution.py:457
  102.8 0.0 slice-start
  102.8 0.1 fusion.15
  102.9 0.1 fusion.5
  103.0 0.1 copy.22
  103.1 0.1 reshape.34.target_ref
  103.2 0.9 slice-done
  104.0 0.7 copy.26
  104.7 1.4 reshape.29
  106.1 7.7 %reduce = f32[4,256,2,256]{3,2,1,0:T(2,128)S(1)} reduce(f32[4,1,256,2,1,256]{5,4,3,2,1,0:T(1,128)} %param.3, f32[]{:T(128)} %constant.69), dimensions={1,4}, to_apply=%get-tuple-element.35.reduce_sub_computation | reduce | bytes 4194308 | tf_op jit(solution)/shard_map/optimization_barrier | solution.py:459
  113.8 1.5 copy.30
  115.3 0.2 broadcast_in_dim.3.start_ref
  115.5 8.0 %child_sum.2.start_ref = f32[1024,512]{1,0:T(8,128)S(1)} custom-call(s32[8,1,512]{2,1,0:T(1,128)S(1)} %reshape.34.target_ref, bf16[128,2,32,256]{3,2,1,0:T(8,128)(2,1)} %all-to-all-done.1.child_ref, f32[1024,512]{1,0:T(8,128)S(1)} %broadcast_in_dim.3.start_ref), custom_call_target="tpu_custom_call" | custom-call | flops 4294967296 | bytes 8388608 | tf_op jit(solution)/shard_map/child_sum/pallas_call | solution.py:211
  123.6 0.0 copy-start.1
  123.6 1.3 copy-done.1
  124.9 31.6 %all-to-all-done.2.child_ref = bf16[128,2,32,256]{3,2,1,0:T(8,128)(2,1)} async-done(((bf16[128,2,32,256]{3,2,1,0:T(8,128)(2,1)}), bf16[128,2,32,256]{3,2,1,0:T(8,128)(2,1)}, u32[]{:S(2)}, u32[]{:S(2)}) %all-to-all-start.2) | async-done | bytes 4194336 | tf_op jit(solution)/shard_map/all_to_all | solution.py:457
  156.4 4.5 %all-to-all-start.3 = ((f32[128,8,256]{2,1,0:T(8,128)}), f32[128,8,256]{2,1,0:T(8,128)S(1)}, u32[]{:S(2)}, u32[]{:S(2)}) async-start(f32[128,8,256]{2,1,0:T(8,128)} %reshape.29), calls=%async_computation.3 | async-start | bytes 2097152 | tf_op jit(solution)/shard_map/all_to_all | solution.py:473
  160.9 0.1 copy.19
  161.0 0.1 reshape.33.target_ref
  161.1 0.6 pad_add_fusion.where_ref
  161.8 1.6 copy-done.2
  163.4 8.1 %child_sum.3.sums_ref = f32[1024,512]{1,0:T(8,128)S(1)} custom-call(s32[8,1,512]{2,1,0:T(1,128)S(1)} %reshape.33.target_ref, bf16[128,2,32,256]{3,2,1,0:T(8,128)(2,1)} %all-to-all-done.2.child_ref, f32[1024,512]{1,0:T(8,128)S(1)} %copy-done.2), custom_call_target="tpu_custom_call" | custom-call | flops 4294967296 | bytes 8388608 | tf_op jit(solution)/shard_map/child_sum/pallas_call | solution.py:211
  171.5 0.0 copy-start
  171.5 1.5 convert_bitcast_fusion
  173.0 13.3 %all-to-all-done.3.base_ref = f32[128,8,256]{2,1,0:T(8,128)S(1)} async-done(((f32[128,8,256]{2,1,0:T(8,128)}), f32[128,8,256]{2,1,0:T(8,128)S(1)}, u32[]{:S(2)}, u32[]{:S(2)}) %all-to-all-start.3) | async-done | bytes 1048608 | tf_op jit(solution)/shard_map/all_to_all | solution.py:473
  186.3 1.0 copy-done.3
  187.3 5.7 %encode.1 = s16[128,4,4992]{2,1,0:T(4,128)(2,1)} custom-call(f32[1024,512]{1,0:T(8,128)} %copy-done, f32[128,8,256]{2,1,0:T(8,128)} %copy-done.3), custom_call_target="tpu_custom_call" | custom-call | bytes 8257536 | tf_op jit(solution)/shard_map/encode/pallas_call | solution.py:234
  193.0 5.6 %all-to-all-start.4 = ((s16[128,4,4992]{2,1,0:T(4,128)(2,1)}), s16[128,4,4992]{2,1,0:T(4,128)(2,1)}, u32[]{:S(2)}, u32[]{:S(2)}) async-start(s16[128,4,4992]{2,1,0:T(4,128)(2,1)} %encode.1), calls=%async_computation.4 | async-start | bytes 10223616 | tf_op jit(solution)/shard_map/all_to_all | solution.py:485
  198.6 0.0 all-gather.2.cloned.1.call-done.a_ref
  198.6 55.4 %leading.1 = (bf16[1536,1536]{1,0:T(8,128)(2,1)}, bf16[1536,1536]{1,0:T(8,128)(2,1)}, bf16[256,1536]{1,0:T(8,128)(2,1)}, bf16[256,1536]{1,0:T(8,128)(2,1)}, f32[256,256]{1,0:T(8,128)}) custom-call(s32[3]{0:T(128)} %pad_add_fusion.where_ref, f32[2048,768]{1,0:T(8,128)} %all-gather.2.cloned.1.call-done.a_ref), custom_call_target="tpu_custom_call" | custom-call | flops 86973087744 | bytes 17563660 | tf_op jit(solution)/shard_map/leading/pallas_call | solution.py:234
  254.0 6.8 %all-to-all-done.4.code_ref = s16[128,4,4992]{2,1,0:T(4,128)(2,1)} async-done(((s16[128,4,4992]{2,1,0:T(4,128)(2,1)}), s16[128,4,4992]{2,1,0:T(4,128)(2,1)}, u32[]{:S(2)}, u32[]{:S(2)}) %all-to-all-start.4) | async-done | bytes 5111840 | tf_op jit(solution)/shard_map/all_to_all | solution.py:485
  260.8 4.7 %all-to-all-start.5 = ((f16[128,8,512]{2,1,0:T(8,128)(2,1)}), f16[128,8,512]{2,1,0:T(8,128)(2,1)S(1)}, u32[]{:S(2)}, u32[]{:S(2)}) async-start(f16[128,8,512]{2,1,0:T(8,128)(2,1)} %convert_bitcast_fusion), calls=%async_computation.5 | async-start | bytes 2097152 | tf_op jit(solution)/shard_map/all_to_all | solution.py:506
  265.5 25.9 %column.1 = (bf16[512,1536]{1,0:T(8,128)(2,1)}, bf16[512,1536]{1,0:T(8,128)(2,1)}) custom-call(s16[128,4,4992]{2,1,0:T(4,128)(2,1)} %all-to-all-done.4.code_ref, bf16[1536,1536]{1,0:T(8,128)(2,1)} %get-tuple-element.46.wh_ref, bf16[1536,1536]{1,0:T(8,128)(2,1)} %get-tuple-element.47.wl_ref), custom_call_target="tpu_custom_call" | custom-call | flops 14495514624 | bytes 17694720 | tf_op jit(solution)/shard_map/column/pallas_call | solution.py:234
  291.4 1.6 convert_element_type.11.sums_ref
  293.0 14.5 %final.1 = f32[4096,128]{1,0:T(8,128)} custom-call(s32[3]{0:T(128)} %pad_add_fusion.where_ref, s16[128,4,4992]{2,1,0:T(4,128)(2,1)} %all-to-all-done.4.code_ref, bf16[512,1536]{1,0:T(8,128)(2,1)} %get-tuple-element.48.gh_ref, bf16[512,1536]{1,0:T(8,128)(2,1)} %get-tuple-element.49.gl_ref, bf16[256,1536]{1,0:T(8,128)(2,1)} %get-tuple-element.50.wh_ref, ...), custom_call_target="tpu_custom_call" | custom-call | flops 4831838208 | bytes 16384012 | tf_op jit(solution)/shard_map/final/pallas_call | solution.py:234
  (12 shorter events, 0.0 us)
Async XLA Ops:
  8.4 20.0 %all-to-all-start = ((f32[16,16,256]{2,1,0:T(8,128)}), f32[16,16,256]{2,1,0:T(8,128)S(1)}, u32[]{:S(2)}, u32[]{:S(2)}) async-start(f32[16,16,256]{2,1,0:T(8,128)} %bitcast.11), calls=%async_computation | async-start | bytes 524288 | tf_op jit(solution)/shard_map/all_to_all | solution.py:442
  16.8 181.8 %all-gather.2.cloned.1.call-start = ((), (), s32[]{:S(2)}) async-start(), calls=%async_computation.6 | async-start | bytes 6340608 | tf_op jit(solution)/shard_map/all_gather | solution.py:452
  28.5 0.7 collective-permute-start
  29.8 67.9 %all-to-all-start.1 = ((bf16[128,2,32,256]{3,2,1,0:T(8,128)(2,1)}), bf16[128,2,32,256]{3,2,1,0:T(8,128)(2,1)}, u32[]{:S(2)}, u32[]{:S(2)}) async-start(bf16[128,2,32,256]{3,2,1,0:T(8,128)(2,1)} %cut_rows.2), calls=%async_computation.1 | async-start | bytes 8388608 | tf_op jit(solution)/shard_map/all_to_all | solution.py:453
  56.6 46.2 %copy-start.4 = (s32[128,64,2]{0,2,1:T(2,128)S(1)}, s32[128,64,2]{0,2,1:T(2,128)}, u32[]{:S(2)}) copy-start(s32[128,64,2]{0,2,1:T(2,128)} %param.5) | copy-start | bytes 196612
  97.7 58.7 %all-to-all-start.2 = ((bf16[128,2,32,256]{3,2,1,0:T(8,128)(2,1)}), bf16[128,2,32,256]{3,2,1,0:T(8,128)(2,1)}, u32[]{:S(2)}, u32[]{:S(2)}) async-start(bf16[128,2,32,256]{3,2,1,0:T(8,128)(2,1)} %cut_rows.3), calls=%async_computation.2 | async-start | bytes 8388608 | tf_op jit(solution)/shard_map/all_to_all | solution.py:457
  102.8 1.2 slice-start
  123.6 1.3 copy-start.1
  156.4 29.8 %all-to-all-start.3 = ((f32[128,8,256]{2,1,0:T(8,128)}), f32[128,8,256]{2,1,0:T(8,128)S(1)}, u32[]{:S(2)}, u32[]{:S(2)}) async-start(f32[128,8,256]{2,1,0:T(8,128)} %reshape.29), calls=%async_computation.3 | async-start | bytes 2097152 | tf_op jit(solution)/shard_map/all_to_all | solution.py:473
  161.8 1.6 copy-start.2
  171.5 14.8 %copy-start = (f32[1024,512]{1,0:T(8,128)}, f32[1024,512]{1,0:T(8,128)S(1)}, u32[]{:S(2)}) copy-start(f32[1024,512]{1,0:T(8,128)S(1)} %child_sum.3.sums_ref) | copy-start | bytes 6291460
  186.3 1.0 copy-start.3
  193.0 67.8 %all-to-all-start.4 = ((s16[128,4,4992]{2,1,0:T(4,128)(2,1)}), s16[128,4,4992]{2,1,0:T(4,128)(2,1)}, u32[]{:S(2)}, u32[]{:S(2)}) async-start(s16[128,4,4992]{2,1,0:T(4,128)(2,1)} %encode.1), calls=%async_computation.4 | async-start | bytes 10223616 | tf_op jit(solution)/shard_map/all_to_all | solution.py:485
  260.8 30.6 %all-to-all-start.5 = ((f16[128,8,512]{2,1,0:T(8,128)(2,1)}), f16[128,8,512]{2,1,0:T(8,128)(2,1)S(1)}, u32[]{:S(2)}, u32[]{:S(2)}) async-start(f16[128,8,512]{2,1,0:T(8,128)(2,1)} %convert_bitcast_fusion), calls=%async_computation.5 | async-start | bytes 2097152 | tf_op jit(solution)/shard_map/all_to_all | solution.py:506
Sparse Core Ops, SparseCore 0:
  29.9 153.9 all-gather.1

commit v3 on v2

--- a/solution.py
+++ b/solution.py
@@ -169,30 +169,29 @@
                 out_ref[d, e, :, across] = rows.astype(BF16)
 
 
-def cut_rows(child, devices, share, shares):
+def cut_rows(child, devices):
     stored, tile, _ = child.shape
-    stored = stored // shares
     deep = tile // devices
-    block = 8
+    block = 16
     return pl.pallas_call(
         cut_kernel,
         out_shape=jax.ShapeDtypeStruct((devices, deep, stored, tile), BF16),
         grid=(devices // block,),
-        in_specs=[pl.BlockSpec((stored, block * deep, tile), lambda g: (share, g, 0))],
+        in_specs=[pl.BlockSpec((stored, block * deep, tile), lambda g: (0, g, 0))],
         out_specs=pl.BlockSpec((block, deep, stored, tile), lambda g: (g, 0, 0, 0)),
         scratch_shapes=[pltpu.VMEM((tile // 128, stored * block * deep, 128), F32)],
         compiler_params=pltpu.CompilerParams(vmem_limit_bytes=58 << 20),
         cost_estimate=pl.CostEstimate(
-            flops=child.size // shares, bytes_accessed=4 * child.size // shares, transcendentals=0
+            flops=child.size, bytes_accessed=4 * child.size, transcendentals=0
         ),
         name="cut_rows",
     )(child)
 
 
-def child_sum_kernel(target_ref, child_ref, start_ref, out_ref):
+def child_sum_kernel(target_ref, child_ref, out_ref):
     @pl.when(pl.program_id(0) == 0)
     def _():
-        out_ref[...] = start_ref[...]
+        out_ref[...] = jnp.zeros_like(out_ref)
 
     sources, pieces, stored, tile = child_ref.shape
     count = sources * stored
@@ -203,11 +202,9 @@
         out_ref[:, e * tile : (e + 1) * tile] += jnp.dot(hot, right, preferred_element_type=F32)
 
 
-def child_sum(target, child, start):
+def child_sum(target, child, tiles):
     devices, pieces, stored, tile = child.shape
-    tiles = start.shape[0]
     block = 512 // stored
-    resident = pl.BlockSpec((tiles, pieces * tile), lambda g: (0, 0))
     return pl.pallas_call(
         child_sum_kernel,
         out_shape=jax.ShapeDtypeStruct((tiles, pieces * tile), F32),
@@ -215,17 +212,16 @@
         in_specs=[
             pl.BlockSpec((1, 1, block * stored), lambda g: (g, 0, 0)),
             pl.BlockSpec((block, pieces, stored, tile), lambda g: (g, 0, 0, 0)),
-            resident,
         ],
-        out_specs=resident,
+        out_specs=pl.BlockSpec((tiles, pieces * tile), lambda g: (0, 0)),
         compiler_params=pltpu.CompilerParams(vmem_limit_bytes=24 << 20),
         cost_estimate=pl.CostEstimate(
             flops=2 * tiles * child.size,
-            bytes_accessed=2 * child.size + 8 * pieces * tiles * tile,
+            bytes_accessed=2 * child.size + 4 * pieces * tiles * tile,
             transcendentals=0,
         ),
         name="child_sum",
-    )(target.reshape(devices // block, 1, block * stored), child, start)
+    )(target.reshape(devices // block, 1, block * stored), child)
 
 
 def whole_call(kernel, name, out_shape, args, scratch=(), scalars=0, limit=58, flops=0):
@@ -436,7 +432,7 @@
     shape = jax.ShapeDtypeStruct
 
     held = child_tiles.reshape(stored, tile, tile)
-    cut = cut_rows(held, devices, 0, 2)
+    cut = cut_rows(held, devices)
 
     mine = parent_front[0, 0, :, 0, 0, :].reshape(col_count, part, tile)
     mine = lax.all_to_all(mine, "col", 0, 0, tiled=True)
@@ -451,27 +447,18 @@
     cut, packed = lax.optimization_barrier((cut, packed))
     packed = lax.all_gather(packed, BOTH, axis=0, tiled=True)
     spread = lax.all_to_all(cut, BOTH, split_axis=0, concat_axis=0, tiled=True)
-    held, _ = lax.optimization_barrier((held, cut))
-    cut = cut_rows(held, devices, 1, 2)
-    cut, spread = lax.optimization_barrier((cut, spread))
-    second = lax.all_to_all(cut, BOTH, split_axis=0, concat_axis=0, tiled=True)
-
     later, _ = lax.optimization_barrier((parent_front, cut))
     base = later[:, 0, :, 0, 0, :].reshape(lrows, devices, deep, tile).transpose(1, 2, 0, 3)
     base = base.reshape(devices, deep * lrows, tile)
     front = later.reshape(lrows * tile, lcols * tile)
-    second, base, front = lax.optimization_barrier((second, base, front))
+    spread, base, front = lax.optimization_barrier((spread, base, front))
 
     rows_all = tile_target[:, :, 0].reshape(-1)
     cols_all = tile_target[:, :, 1].reshape(-1)
     owner = rows_all % row_count * col_count + cols_all % col_count
     target = owner * slots + cols_all // col_count * lrows + rows_all // row_count
-    target = target.reshape(devices, stored)
-    sums = jnp.zeros((devices * slots, deep * tile), F32)
-    sums = child_sum(target[:, : stored // 2], spread, sums)
-    second, sums, base = lax.optimization_barrier((second, sums, base))
     base = lax.all_to_all(base, BOTH, split_axis=0, concat_axis=0, tiled=True)
-    sums = child_sum(target[:, stored // 2 :], second, sums)
+    sums = child_sum(target, spread, devices * slots)
 
     (to_both,) = whole_call(
         functools.partial(encode_kernel, PANELS, row_count, deep),
@@ -479,6 +466,7 @@
         [shape((devices, lrows, (deep + 1) * (order + lanes)), jnp.int16)],
         [sums, base],
         scratch=[pltpu.VMEM((groups + 1, deep * lrows, lanes), F32)],
+        limit=32,
     )
     to_owner = sums.reshape(devices, slots, deep * tile).astype(F16)
     packed, _ = lax.optimization_barrier((packed, to_both))

time: 316 us -> 305 us (0.965)
  Pallas kernels: 141 us -> 127 us
  waiting for transfers between devices: 92.9 us -> 96.2 us
    all_to_all x1, waiting for transfers between devices: 41.1 us -> 87.4 us  [shards(): spread = lax.all_to_all(cut, BOTH, split_axis=0, concat_axis=0, tiled=True)]
    all_to_all x1 -> x0, waiting for transfers between devices: 31.6 us -> none  [shards(): second = lax.all_to_all(cut, BOTH, split_axis=0, concat_axis=0, tiled=True)]
    all_to_all x1, waiting for transfers between devices: 13.3 us -> 2.2 us  [shards(): base = lax.all_to_all(base, BOTH, split_axis=0, concat_axis=0, tiled=True)]
    pallas_call x2 -> x1, Pallas kernels: 23 us -> 14.1 us  [cut_rows(): pl.pallas_call(cut_kernel, out_shape=jax.ShapeDtypeStruct((devices, deep,...]
    all_to_all x1, starting transfers between devices: 4.46 us -> 9.95 us  [shards(): base = lax.all_to_all(base, BOTH, split_axis=0, concat_axis=0, tiled=True)]
    all_to_all x1 -> x0, starting transfers between devices: 5.08 us -> none  [shards(): second = lax.all_to_all(cut, BOTH, split_axis=0, concat_axis=0, tiled=True)]
    pallas_call x4, Pallas kernels: 102 us -> 97.5 us  [whole_call(): pl.pallas_call(kernel, out_shape=out_shape, in_specs=[pl.BlockSpec(memory...]
    all_to_all x1, waiting for transfers between devices: 6.8 us -> 3.47 us  [shards(): lax.all_to_all(to_both, BOTH, split_axis=0, concat_axis=0, tiled=True)]
  transfers between devices with their start and end apart: 8 -> 7, of which waited for: 4 -> 4; matrix products, arithmetic and copies ran while one was open for 4% -> 5% of each run, Pallas kernels for 40% -> 37%
where the time goes in v3:
time: 305 us; the launch traced here: 304 us
  Pallas kernels  127 us (42%)
  waiting for transfers between devices  96.2 us (32%)
  starting transfers between devices  47 us (15%)
  between operations  13.6 us (4%)
  other arithmetic  12.3 us (4%)
  local copies, waits for them, and re-layouts  8.09 us (3%)
    pallas_call x4, Pallas kernels, whole_call(): pl.pallas_call(kernel, out_shape=out_shape, in_specs=[pl.BlockSpec(memory...  97.5 us
    all_to_all x1, waiting for transfers between devices, shards(): spread = lax.all_to_all(cut, BOTH, split_axis=0, concat_axis=0, tiled=True)  87.4 us
    all_to_all x1, starting transfers between devices, shards(): spread = lax.all_to_all(cut, BOTH, split_axis=0, concat_axis=0, tiled=True)  15.3 us
    pallas_call x1, Pallas kernels, child_sum(): pl.pallas_call(child_sum_kernel, out_shape=jax.ShapeDtypeStruct((tiles, p...  15.2 us
    pallas_call x1, Pallas kernels, cut_rows(): pl.pallas_call(cut_kernel, out_shape=jax.ShapeDtypeStruct((devices, deep,...  14.1 us
    all_to_all x1, starting transfers between devices, shards(): base = lax.all_to_all(base, BOTH, split_axis=0, concat_axis=0, tiled=True)  9.95 us
    all_to_all x1, starting transfers between devices, shards(): mine = lax.all_to_all(mine, 'col', 0, 0, tiled=True)  8.43 us
    all_to_all x1, starting transfers between devices, shards(): lax.all_to_all(to_both, BOTH, split_axis=0, concat_axis=0, tiled=True)  7.97 us
  transfers between devices with their start and end apart: 7, of which 4 were waited for; matrix products, arithmetic and copies ran while one was open for 5% of the time, Pallas kernels for 37%

profile of v3, /device:TPU:1, one launch (start us, length us, event | category | flops | bytes accessed | tf_op | source)
XLA Modules:
  0.0 304.0 jit_solution(8629617049237551918)
XLA Ops:
  6.5 1.1 slice.29
  7.7 0.7 copy.36
  8.4 8.4 %all-to-all-start = ((f32[16,16,256]{2,1,0:T(8,128)}), f32[16,16,256]{2,1,0:T(8,128)S(1)}, u32[]{:S(2)}, u32[]{:S(2)}) async-start(f32[16,16,256]{2,1,0:T(8,128)} %bitcast.9), calls=%async_computation | async-start | bytes 524288 | tf_op jit(solution)/shard_map/all_to_all | solution.py:438
  16.8 0.0 all-gather.2.cloned.1.call-start
  16.9 14.1 %cut_rows.1 = bf16[128,2,64,256]{3,2,1,0:T(8,128)(2,1)} custom-call(bf16[64,256,256]{2,1,0:T(8,128)(2,1)} %bitcast.21), custom_call_target="tpu_custom_call" | custom-call | flops 4194304 | bytes 16777216 | tf_op jit(solution)/shard_map/cut_rows/pallas_call | solution.py:176
  30.9 0.0 all-to-all-done
  31.0 0.7 collective-permute-start
  31.7 0.0 collective-permute-done
  31.7 0.6 fusion
  32.3 0.0 all-gather.2.cloned.1.call-update
  32.3 0.0 copy-start.1
  32.4 15.3 %all-to-all-start.1 = ((bf16[128,2,64,256]{3,2,1,0:T(8,128)(2,1)}), bf16[128,2,64,256]{3,2,1,0:T(8,128)(2,1)}, u32[]{:S(2)}, u32[]{:S(2)}) async-start(bf16[128,2,64,256]{3,2,1,0:T(8,128)(2,1)} %cut_rows.1), calls=%async_computation.1 | async-start | bytes 16777216 | tf_op jit(solution)/shard_map/all_to_all | solution.py:449
  47.6 0.0 slice-start
  47.6 0.0 copy-done.1
  47.7 0.1 fusion.3
  47.7 0.1 copy.22
  47.8 0.1 reshape_squeeze.16
  47.9 0.1 copy.26
  48.0 0.1 reshape_squeeze.17
  48.1 0.7 pad_add_fusion.where_ref
  48.8 0.5 add_add_fusion.target_ref
  49.3 0.0 slice-done
  49.3 0.7 copy.35
  50.0 1.3 reshape.228
  51.3 7.7 %reduce = f32[4,256,2,256]{3,2,1,0:T(2,128)S(1)} reduce(f32[4,1,256,2,1,256]{5,4,3,2,1,0:T(1,128)} %param.3, f32[]{:T(128)} %constant.67), dimensions={1,4}, to_apply=%get-tuple-element.27.reduce_sub_computation | reduce | bytes 4194308 | tf_op jit(solution)/shard_map/optimization_barrier | solution.py:450
  59.0 1.5 copy.38
  60.5 87.4 %all-to-all-done.1.child_ref = bf16[128,2,64,256]{3,2,1,0:T(8,128)(2,1)} async-done(((bf16[128,2,64,256]{3,2,1,0:T(8,128)(2,1)}), bf16[128,2,64,256]{3,2,1,0:T(8,128)(2,1)}, u32[]{:S(2)}, u32[]{:S(2)}) %all-to-all-start.1) | async-done | bytes 8388640 | tf_op jit(solution)/shard_map/all_to_all | solution.py:449
  147.9 9.9 %all-to-all-start.2 = ((f32[128,8,256]{2,1,0:T(8,128)}), f32[128,8,256]{2,1,0:T(8,128)S(1)}, u32[]{:S(2)}, u32[]{:S(2)}) async-start(f32[128,8,256]{2,1,0:T(8,128)} %reshape.228), calls=%async_computation.2 | async-start | bytes 2097152 | tf_op jit(solution)/shard_map/all_to_all | solution.py:460
  157.8 15.2 %child_sum.1.sums_ref = f32[1024,512]{1,0:T(8,128)S(1)} custom-call(s32[16,1,512]{2,1,0:T(1,128)S(1)} %add_add_fusion.target_ref, bf16[128,2,64,256]{3,2,1,0:T(8,128)(2,1)} %all-to-all-done.1.child_ref), custom_call_target="tpu_custom_call" | custom-call | flops 8589934592 | bytes 10485760 | tf_op jit(solution)/shard_map/child_sum/pallas_call | solution.py:208
  173.1 1.2 convert_bitcast_fusion
  174.3 2.2 all-to-all-done.2.base_ref
  176.5 1.6 encode.1
  178.1 0.0 copy-start
  178.1 2.2 copy-done
  180.3 8.0 %all-to-all-start.3 = ((s16[128,4,4992]{2,1,0:T(4,128)(2,1)}), s16[128,4,4992]{2,1,0:T(4,128)(2,1)}, u32[]{:S(2)}, u32[]{:S(2)}) async-start(s16[128,4,4992]{2,1,0:T(4,128)(2,1)} %copy-done), calls=%async_computation.3 | async-start | bytes 10223616 | tf_op jit(solution)/shard_map/all_to_all | solution.py:473
  188.3 3.2 %all-gather.2.cloned.1.call-done.a_ref = f32[2048,768]{1,0:T(8,128)} async-done(((f32[16,768]{1,0:T(8,128)}), f32[2048,768]{1,0:T(8,128)}) %all-gather.2.cloned.1.call-update) | async-done | bytes 6291472 | tf_op jit(solution)/shard_map/all_gather | solution.py:448
  191.5 55.5 %leading.1 = (bf16[1536,1536]{1,0:T(8,128)(2,1)}, bf16[1536,1536]{1,0:T(8,128)(2,1)}, bf16[256,1536]{1,0:T(8,128)(2,1)}, bf16[256,1536]{1,0:T(8,128)(2,1)}, f32[256,256]{1,0:T(8,128)}) custom-call(s32[3]{0:T(128)} %pad_add_fusion.where_ref, f32[2048,768]{1,0:T(8,128)} %all-gather.2.cloned.1.call-done.a_ref), custom_call_target="tpu_custom_call" | custom-call | flops 86973087744 | bytes 17563660 | tf_op jit(solution)/shard_map/leading/pallas_call | solution.py:230
  247.0 3.5 %all-to-all-done.3.code_ref = s16[128,4,4992]{2,1,0:T(4,128)(2,1)} async-done(((s16[128,4,4992]{2,1,0:T(4,128)(2,1)}), s16[128,4,4992]{2,1,0:T(4,128)(2,1)}, u32[]{:S(2)}, u32[]{:S(2)}) %all-to-all-start.3) | async-done | bytes 5111840 | tf_op jit(solution)/shard_map/all_to_all | solution.py:473
  250.5 4.7 %all-to-all-start.4 = ((f16[128,8,512]{2,1,0:T(8,128)(2,1)}), f16[128,8,512]{2,1,0:T(8,128)(2,1)S(1)}, u32[]{:S(2)}, u32[]{:S(2)}) async-start(f16[128,8,512]{2,1,0:T(8,128)(2,1)} %convert_bitcast_fusion), calls=%async_computation.4 | async-start | bytes 2097152 | tf_op jit(solution)/shard_map/all_to_all | solution.py:494
  255.1 25.9 %column.1 = (bf16[512,1536]{1,0:T(8,128)(2,1)}, bf16[512,1536]{1,0:T(8,128)(2,1)}) custom-call(s16[128,4,4992]{2,1,0:T(4,128)(2,1)} %all-to-all-done.3.code_ref, bf16[1536,1536]{1,0:T(8,128)(2,1)} %get-tuple-element.34.wh_ref, bf16[1536,1536]{1,0:T(8,128)(2,1)} %get-tuple-element.35.wl_ref), custom_call_target="tpu_custom_call" | custom-call | flops 14495514624 | bytes 17694720 | tf_op jit(solution)/shard_map/column/pallas_call | solution.py:230
  281.0 0.0 all-to-all-done.4
  281.0 1.6 convert_element_type.11.sums_ref
  282.6 14.5 %final.1 = f32[4096,128]{1,0:T(8,128)} custom-call(s32[3]{0:T(128)} %pad_add_fusion.where_ref, s16[128,4,4992]{2,1,0:T(4,128)(2,1)} %all-to-all-done.3.code_ref, bf16[512,1536]{1,0:T(8,128)(2,1)} %get-tuple-element.36.gh_ref, bf16[512,1536]{1,0:T(8,128)(2,1)} %get-tuple-element.37.gl_ref, bf16[256,1536]{1,0:T(8,128)(2,1)} %get-tuple-element.38.wh_ref, ...), custom_call_target="tpu_custom_call" | custom-call | flops 4831838208 | bytes 16384012 | tf_op jit(solution)/shard_map/final/pallas_call | solution.py:230
  (5 shorter events, 0.0 us)
Async XLA Ops:
  8.4 22.5 %all-to-all-start = ((f32[16,16,256]{2,1,0:T(8,128)}), f32[16,16,256]{2,1,0:T(8,128)S(1)}, u32[]{:S(2)}, u32[]{:S(2)}) async-start(f32[16,16,256]{2,1,0:T(8,128)} %bitcast.9), calls=%async_computation | async-start | bytes 524288 | tf_op jit(solution)/shard_map/all_to_all | solution.py:438
  16.8 174.7 %all-gather.2.cloned.1.call-start = ((), (), s32[]{:S(2)}) async-start(), calls=%async_computation.5 | async-start | bytes 6340608 | tf_op jit(solution)/shard_map/all_gather | solution.py:448
  31.0 0.7 collective-permute-start
  32.3 15.3 %copy-start.1 = (s32[128,64,2]{0,2,1:T(2,128)S(1)}, s32[128,64,2]{0,2,1:T(2,128)}, u32[]{:S(2)}) copy-start(s32[128,64,2]{0,2,1:T(2,128)} %param.5) | copy-start | bytes 196612
  32.4 115.5 %all-to-all-start.1 = ((bf16[128,2,64,256]{3,2,1,0:T(8,128)(2,1)}), bf16[128,2,64,256]{3,2,1,0:T(8,128)(2,1)}, u32[]{:S(2)}, u32[]{:S(2)}) async-start(bf16[128,2,64,256]{3,2,1,0:T(8,128)(2,1)} %cut_rows.1), calls=%async_computation.1 | async-start | bytes 16777216 | tf_op jit(solution)/shard_map/all_to_all | solution.py:449
  47.6 1.7 slice-start
  147.9 28.6 %all-to-all-start.2 = ((f32[128,8,256]{2,1,0:T(8,128)}), f32[128,8,256]{2,1,0:T(8,128)S(1)}, u32[]{:S(2)}, u32[]{:S(2)}) async-start(f32[128,8,256]{2,1,0:T(8,128)} %reshape.228), calls=%async_computation.2 | async-start | bytes 2097152 | tf_op jit(solution)/shard_map/all_to_all | solution.py:460
  178.1 2.2 copy-start
  180.3 70.1 %all-to-all-start.3 = ((s16[128,4,4992]{2,1,0:T(4,128)(2,1)}), s16[128,4,4992]{2,1,0:T(4,128)(2,1)}, u32[]{:S(2)}, u32[]{:S(2)}) async-start(s16[128,4,4992]{2,1,0:T(4,128)(2,1)} %copy-done), calls=%async_computation.3 | async-start | bytes 10223616 | tf_op jit(solution)/shard_map/all_to_all | solution.py:473
  250.5 30.5 %all-to-all-start.4 = ((f16[128,8,512]{2,1,0:T(8,128)(2,1)}), f16[128,8,512]{2,1,0:T(8,128)(2,1)S(1)}, u32[]{:S(2)}, u32[]{:S(2)}) async-start(f16[128,8,512]{2,1,0:T(8,128)(2,1)} %convert_bitcast_fusion), calls=%async_computation.4 | async-start | bytes 2097152 | tf_op jit(solution)/shard_map/all_to_all | solution.py:494
Sparse Core Ops, SparseCore 0:
  32.5 158.9 all-gather.1

commit v4 on v3

--- a/solution.py
+++ b/solution.py
@@ -54,8 +54,6 @@
     a_ref,
     high_ref,
     low_ref,
-    own_high_ref,
-    own_low_ref,
     top_ref,
     l_ref,
     lh_ref,
@@ -152,8 +150,6 @@
 
     r = jnp.minimum(where_ref[0], panels - 1)
     c = jnp.minimum(where_ref[1], panels - 1)
-    own_high_ref[...] = high_ref[at(c), :]
-    own_low_ref[...] = low_ref[at(c), :]
     top_ref[...] = l_ref[at(r), at(c)]
 
 
@@ -240,7 +236,9 @@
     )(*args)
 
 
-def encode_kernel(panels, rows, deep, sums_ref, base_ref, out_ref, x_ref):
+def encode_kernel(
+    panels, rows, deep, sums_ref, base_ref, out_ref, x_ref, row_ref, col_ref
+):
     devices, wide, tile = base_ref.shape
     cols = devices // rows
     slots = sums_ref.shape[0] // devices
@@ -248,10 +246,10 @@
     lanes = 128
     each = tile // lanes
     groups = panels * each
-    coded = (groups + 1) * lanes
+    coded = groups * lanes
     lane = lax.broadcasted_iota(jnp.int32, (wide, lanes), 1)
     for r in range(rows):
-        powers = jnp.zeros((wide, lanes), F32)
+        powers = [jnp.zeros((wide, lanes), F32)] * (deep + 1)
         for k in range(panels):
             first = (r * cols + k) * slots
             child = [
@@ -262,11 +260,17 @@
             power = jnp.floor(jnp.log(top) * 1.4426950408889634) + 1.0
             code = jnp.round(x * jnp.exp2(15.0 - power))
             code = jnp.clip(code, -32767.0, 32767.0)
-            powers = jnp.where(lane == k, power, powers)
+            powers = [jnp.where(lane == n * panels + k, power, p) for n, p in enumerate(powers)]
             for h in range(each):
                 x_ref[k * each + h] = code[:, h * lanes : (h + 1) * lanes]
-        x_ref[groups] = powers
-        for g in range(groups + 1):
+        for n in range(deep):
+            power = powers[n][n * lrows : (n + 1) * lrows, :]
+            row_power = power if n == 0 else row_power + power
+        row_ref[r] = row_power
+        x_ref[groups] = powers[deep]
+        for u in range(cols // rows):
+            col_ref[u * rows + r] = x_ref[groups, pl.ds(u, lrows, stride=wide // lrows), :]
+        for g in range(groups):
             across = [slice(n * coded + g * lanes, n * coded + (g + 1) * lanes) for n in range(deep + 1)]
             for e in range(deep):
                 piece = x_ref[g, e * lrows : (e + 1) * lrows, :]
@@ -278,37 +282,56 @@
                 some = some.astype(jnp.int32).astype(jnp.int16)
                 for m in range(rows):
                     out_ref[m * cols + u * rows + r, :, across[deep]] = some
-
-
-def spread_rows(raw_ref, first, out_ref, source, step, count, target, tile):
-    lanes = 128
-    each = tile // lanes
+    for m in range(rows):
+        for c in range(cols):
+            power = (row_ref[m] + col_ref[c]).astype(jnp.int32).astype(jnp.int16)
+            out_ref[m * cols + c, :, (deep + 1) * coded :] = power
+
+
+def spread_rows(raw_ref, part, panels, out_ref, source, step, count, target):
     groups = out_ref.shape[0]
-    scale = jnp.exp2(raw_ref[first + groups, pl.ds(source, count, stride=step), :] - 15.0)
+    last = raw_ref.shape[0] - 1
+    scale = jnp.exp2(raw_ref[last, pl.ds(source, count, stride=step), :] - 15.0)
     for g in range(groups):
-        k = g // each
-        x = raw_ref[first + g, pl.ds(source, count, stride=step), :] * scale[:, k : k + 1]
+        k = part[1] * panels + g // (groups // panels)
+        x = raw_ref[part[0] * groups + g, pl.ds(source, count, stride=step), :] * scale[:, k : k + 1]
         out_ref[g, pl.ds(target, count, stride=2), :] = x
 
 
 def widen(code_ref, first, raw_ref):
     lanes = 128
-    for g in range(raw_ref.shape[0]):
-        across = slice(first + g * lanes, first + (g + 1) * lanes)
+    last = raw_ref.shape[0] - 1
+    for g in range(last + 1):
+        start = code_ref.shape[2] - lanes if g == last else first + g * lanes
+        across = slice(start, start + lanes)
         raw_ref[g] = code_ref[:, :, across].astype(jnp.int32).astype(F32).reshape(raw_ref.shape[1:])
 
 
 def column_kernel(
-    tile, panels, code_ref, wh_ref, wl_ref, gh_ref, gl_ref, raw_ref, nat_ref, xh_ref, xl_ref, acc_ref
+    tile,
+    panels,
+    where_ref,
+    code_ref,
+    wh_ref,
+    wl_ref,
+    gh_ref,
+    gl_ref,
+    raw_ref,
+    nat_ref,
+    xh_ref,
+    xl_ref,
+    acc_ref,
 ):
     at = functools.partial(tile_at, tile)
     devices, pieces, wide = code_ref.shape
     lcols = xh_ref.shape[1] // tile
     each = tile // 128
+    deep = pieces // lcols
     widen(code_ref, wide - raw_ref.shape[0] * 128, raw_ref)
-    for e in range(pieces // lcols):
+    for e in range(deep):
         for j in range(lcols):
-            spread_rows(raw_ref, 0, nat_ref, e * lcols + j, pieces, devices, j * tile + e, tile)
+            source, target = e * lcols + j, j * tile + e
+            spread_rows(raw_ref, (0, deep), panels, nat_ref, source, pieces, devices, target)
     for k in range(panels):
         x = jnp.concatenate([nat_ref[k * each + h] for h in range(each)], axis=1)
         xh_ref[k], xl_ref[k] = split(x)
@@ -337,6 +360,14 @@
             )
 
         gh_ref[:, at(j)], gl_ref[:, at(j)] = split(acc_ref[...])
+
+    my_col = where_ref[1]
+
+    @pl.when(my_col < panels)
+    def _():
+        own = at(jnp.minimum(my_col, panels - 1))
+        gh_ref[:tile] = wh_ref[own, :]
+        gl_ref[:tile] = wl_ref[own, :]
 
 
 def final_kernel(
@@ -346,16 +377,12 @@
     code_ref,
     gh_ref,
     gl_ref,
-    wh_ref,
-    wl_ref,
     top_ref,
     sums_ref,
     front_ref,
     out_ref,
     raw_ref,
     nat_ref,
-    bh_ref,
-    bl_ref,
     sum_ref,
     add_ref,
 ):
@@ -365,7 +392,7 @@
     lrows = front_ref.shape[0] // tile
     lcols = front_ref.shape[1] // tile
     groups = nat_ref.shape[0]
-    deep = raw_ref.shape[0] // (groups + 1)
+    deep = sums_ref.shape[2] // tile
     my_row = where_ref[0]
     my_col = where_ref[1]
     row_count = where_ref[2]
@@ -373,19 +400,12 @@
     widen(code_ref, 0, raw_ref)
     for g in range(deep * each):
         sum_ref[g] = sums_ref[:, :, g * lanes : (g + 1) * lanes].reshape(sum_ref.shape[1:])
-    bh_ref[...] = gh_ref[...]
-    bl_ref[...] = gl_ref[...]
-
-    @pl.when(factored)
-    def _():
-        bh_ref[:tile] = wh_ref[...]
-        bl_ref[:tile] = wl_ref[...]
 
     @pl.loop(0, lrows)
     def _(i):
         rows = tile_at(tile, i)
         for e in range(deep):
-            spread_rows(raw_ref, e * (groups + 1), nat_ref, i, pieces, devices, e, tile)
+            spread_rows(raw_ref, (e, e), panels, nat_ref, i, pieces, devices, e)
             for j in range(lcols):
                 for h in range(each):
                     add_ref[j * each + h, pl.ds(e, devices, stride=2), :] = sum_ref[
@@ -396,7 +416,7 @@
         leading = my_row + row_count * i < panels
         for j in range(lcols):
             here = slice(j * tile, (j + 1) * tile)
-            product = three(ah, al, bh_ref[here], bl_ref[here], NT)
+            product = three(ah, al, gh_ref[here], gl_ref[here], NT)
             child = jnp.concatenate([add_ref[j * each + h] for h in range(each)], axis=1)
             value = front_ref[rows, here] + child - product
             cleared = jnp.zeros_like(value)
@@ -463,19 +483,22 @@
     (to_both,) = whole_call(
         functools.partial(encode_kernel, PANELS, row_count, deep),
         "encode",
-        [shape((devices, lrows, (deep + 1) * (order + lanes)), jnp.int16)],
+        [shape((devices, lrows, (deep + 1) * order + lanes), jnp.int16)],
         [sums, base],
-        scratch=[pltpu.VMEM((groups + 1, deep * lrows, lanes), F32)],
+        scratch=[
+            pltpu.VMEM((groups + 1, deep * lrows, lanes), F32),
+            pltpu.VMEM((row_count, lrows, lanes), F32),
+            pltpu.VMEM((col_count, lrows, lanes), F32),
+        ],
         limit=32,
     )
     to_owner = sums.reshape(devices, slots, deep * tile).astype(F16)
     packed, _ = lax.optimization_barrier((packed, to_both))
     both = lax.all_to_all(to_both, BOTH, split_axis=0, concat_axis=0, tiled=True)
-    *inverse, own_high, own_low, top = whole_call(
+    *inverse, top = whole_call(
         functools.partial(leading_kernel, tile, PANELS, places),
         "leading",
         [shape((order, order), BF16)] * 2
-        + [shape((tile, order), BF16)] * 2
         + [shape((tile, tile), F32)],
         [where, packed],
         scratch=[
@@ -497,7 +520,8 @@
         functools.partial(column_kernel, tile, PANELS),
         "column",
         [shape((lcols * tile, order), BF16)] * 2,
-        [both, *inverse],
+        [where, both, *inverse],
+        scalars=1,
         scratch=[
             pltpu.VMEM((groups + 1, lcols * tile, lanes), F32),
             pltpu.VMEM((groups, lcols * tile, lanes), F32),
@@ -512,12 +536,10 @@
         functools.partial(final_kernel, tile, PANELS),
         "final",
         [shape((front.size // lanes, lanes), F32)],
-        [where, both, *right, own_high, own_low, top, summed.astype(F32), front],
+        [where, both, *right, top, summed.astype(F32), front],
         scratch=[
-            pltpu.VMEM((deep * (groups + 1), devices * lrows, lanes), F32),
+            pltpu.VMEM((deep * groups + 1, devices * lrows, lanes), F32),
             pltpu.VMEM((groups, tile, lanes), F32),
-            pltpu.VMEM((lcols * tile, order), BF16),
-            pltpu.VMEM((lcols * tile, order), BF16),
             pltpu.VMEM((deep * tile // lanes, devices * slots, lanes), F32),
             pltpu.VMEM((lcols * tile // lanes, tile, lanes), F32),
         ],

time: 305 us -> 302 us (level)
  no operation moved by 1% of the time
where the time goes in v4:
time: 302 us; the launch traced here: 301 us
  Pallas kernels  126 us (42%)
  waiting for transfers between devices  93.8 us (31%)
  starting transfers between devices  47.8 us (16%)
  between operations  13.6 us (5%)
  other arithmetic  12.3 us (4%)
  local copies, waits for them, and re-layouts  8.16 us (3%)
    pallas_call x4, Pallas kernels, whole_call(): pl.pallas_call(kernel, out_shape=out_shape, in_specs=[pl.BlockSpec(memory...  96.3 us
    all_to_all x1, waiting for transfers between devices, shards(): spread = lax.all_to_all(cut, BOTH, split_axis=0, concat_axis=0, tiled=True)  87.3 us
    all_to_all x1, starting transfers between devices, shards(): spread = lax.all_to_all(cut, BOTH, split_axis=0, concat_axis=0, tiled=True)  15.3 us
    pallas_call x1, Pallas kernels, child_sum(): pl.pallas_call(child_sum_kernel, out_shape=jax.ShapeDtypeStruct((tiles, p...  15.2 us
    pallas_call x1, Pallas kernels, cut_rows(): pl.pallas_call(cut_kernel, out_shape=jax.ShapeDtypeStruct((devices, deep,...  14.1 us
    all_to_all x1, starting transfers between devices, shards(): base = lax.all_to_all(base, BOTH, split_axis=0, concat_axis=0, tiled=True)  9.95 us
    all_to_all x1, starting transfers between devices, shards(): mine = lax.all_to_all(mine, 'col', 0, 0, tiled=True)  8.43 us
    all_to_all x1, starting transfers between devices, shards(): lax.all_to_all(to_both, BOTH, split_axis=0, concat_axis=0, tiled=True)  7.98 us
  transfers between devices with their start and end apart: 7, of which 4 were waited for; matrix products, arithmetic and copies ran while one was open for 5% of the time, Pallas kernels for 37%

profile of v4, /device:TPU:1, one launch (start us, length us, event | category | flops | bytes accessed | tf_op | source)
XLA Modules:
  0.0 301.3 jit_solution(1379969238617840438)
XLA Ops:
  6.5 1.1 slice.29
  7.7 0.7 copy.36
  8.4 8.4 %all-to-all-start = ((f32[16,16,256]{2,1,0:T(8,128)}), f32[16,16,256]{2,1,0:T(8,128)S(1)}, u32[]{:S(2)}, u32[]{:S(2)}) async-start(f32[16,16,256]{2,1,0:T(8,128)} %bitcast.9), calls=%async_computation | async-start | bytes 524288 | tf_op jit(solution)/shard_map/all_to_all | solution.py:458
  16.8 0.0 all-gather.2.cloned.1.call-start
  16.9 14.1 %cut_rows.1 = bf16[128,2,64,256]{3,2,1,0:T(8,128)(2,1)} custom-call(bf16[64,256,256]{2,1,0:T(8,128)(2,1)} %bitcast.21), custom_call_target="tpu_custom_call" | custom-call | flops 4194304 | bytes 16777216 | tf_op jit(solution)/shard_map/cut_rows/pallas_call | solution.py:172
  30.9 0.0 all-to-all-done
  31.0 0.7 collective-permute-start
  31.7 0.0 collective-permute-done
  31.7 0.6 fusion
  32.3 0.0 all-gather.2.cloned.1.call-update
  32.4 0.0 copy-start.1
  32.4 15.3 %all-to-all-start.1 = ((bf16[128,2,64,256]{3,2,1,0:T(8,128)(2,1)}), bf16[128,2,64,256]{3,2,1,0:T(8,128)(2,1)}, u32[]{:S(2)}, u32[]{:S(2)}) async-start(bf16[128,2,64,256]{3,2,1,0:T(8,128)(2,1)} %cut_rows.1), calls=%async_computation.1 | async-start | bytes 16777216 | tf_op jit(solution)/shard_map/all_to_all | solution.py:469
  47.6 0.0 slice-start
  47.7 0.0 copy-done.1
  47.7 0.1 fusion.3
  47.7 0.1 copy.22
  47.8 0.1 reshape_squeeze.16
  47.9 0.1 copy.26
  48.0 0.1 reshape_squeeze.17
  48.1 0.6 pad_add_fusion.where_ref
  48.8 0.5 add_add_fusion.target_ref
  49.3 0.0 slice-done
  49.3 0.7 copy.35
  50.0 1.3 reshape.228
  51.3 7.7 %reduce = f32[4,256,2,256]{3,2,1,0:T(2,128)S(1)} reduce(f32[4,1,256,2,1,256]{5,4,3,2,1,0:T(1,128)} %param.3, f32[]{:T(128)} %constant.67), dimensions={1,4}, to_apply=%get-tuple-element.25.reduce_sub_computation | reduce | bytes 4194308 | tf_op jit(solution)/shard_map/optimization_barrier | solution.py:470
  59.0 1.6 copy.38
  60.6 87.3 %all-to-all-done.1.child_ref = bf16[128,2,64,256]{3,2,1,0:T(8,128)(2,1)} async-done(((bf16[128,2,64,256]{3,2,1,0:T(8,128)(2,1)}), bf16[128,2,64,256]{3,2,1,0:T(8,128)(2,1)}, u32[]{:S(2)}, u32[]{:S(2)}) %all-to-all-start.1) | async-done | bytes 8388640 | tf_op jit(solution)/shard_map/all_to_all | solution.py:469
  147.9 9.9 %all-to-all-start.2 = ((f32[128,8,256]{2,1,0:T(8,128)}), f32[128,8,256]{2,1,0:T(8,128)S(1)}, u32[]{:S(2)}, u32[]{:S(2)}) async-start(f32[128,8,256]{2,1,0:T(8,128)} %reshape.228), calls=%async_computation.2 | async-start | bytes 2097152 | tf_op jit(solution)/shard_map/all_to_all | solution.py:480
  157.9 15.2 %child_sum.1.sums_ref = f32[1024,512]{1,0:T(8,128)S(1)} custom-call(s32[16,1,512]{2,1,0:T(1,128)S(1)} %add_add_fusion.target_ref, bf16[128,2,64,256]{3,2,1,0:T(8,128)(2,1)} %all-to-all-done.1.child_ref), custom_call_target="tpu_custom_call" | custom-call | flops 8589934592 | bytes 10485760 | tf_op jit(solution)/shard_map/child_sum/pallas_call | solution.py:204
  173.1 1.2 convert_bitcast_fusion
  174.3 2.2 all-to-all-done.2.base_ref
  176.5 1.6 encode.1
  178.1 0.0 copy-start
  178.1 2.2 copy-done
  180.3 8.0 %all-to-all-start.3 = ((s16[128,4,4736]{2,1,0:T(4,128)(2,1)}), s16[128,4,4736]{2,1,0:T(4,128)(2,1)}, u32[]{:S(2)}, u32[]{:S(2)}) async-start(s16[128,4,4736]{2,1,0:T(4,128)(2,1)} %copy-done), calls=%async_computation.3 | async-start | bytes 9699328 | tf_op jit(solution)/shard_map/all_to_all | solution.py:497
  188.3 3.2 %all-gather.2.cloned.1.call-done.a_ref = f32[2048,768]{1,0:T(8,128)} async-done(((f32[16,768]{1,0:T(8,128)}), f32[2048,768]{1,0:T(8,128)}) %all-gather.2.cloned.1.call-update) | async-done | bytes 6291472 | tf_op jit(solution)/shard_map/all_gather | solution.py:468
  191.5 55.0 %leading.1 = (bf16[1536,1536]{1,0:T(8,128)(2,1)}, bf16[1536,1536]{1,0:T(8,128)(2,1)}, f32[256,256]{1,0:T(8,128)}) custom-call(s32[3]{0:T(128)} %pad_add_fusion.where_ref, f32[2048,768]{1,0:T(8,128)} %all-gather.2.cloned.1.call-done.a_ref), custom_call_target="tpu_custom_call" | custom-call | flops 86973087744 | bytes 15990796 | tf_op jit(solution)/shard_map/leading/pallas_call | solution.py:226
  246.5 1.1 all-to-all-done.3.code_ref
  247.6 5.5 %all-to-all-start.4 = ((f16[128,8,512]{2,1,0:T(8,128)(2,1)}), f16[128,8,512]{2,1,0:T(8,128)(2,1)S(1)}, u32[]{:S(2)}, u32[]{:S(2)}) async-start(f16[128,8,512]{2,1,0:T(8,128)(2,1)} %convert_bitcast_fusion), calls=%async_computation.4 | async-start | bytes 2097152 | tf_op jit(solution)/shard_map/all_to_all | solution.py:517
  253.1 26.2 %column.1 = (bf16[512,1536]{1,0:T(8,128)(2,1)}, bf16[512,1536]{1,0:T(8,128)(2,1)}) custom-call(s32[3]{0:T(128)} %pad_add_fusion.where_ref, s16[128,4,4736]{2,1,0:T(4,128)(2,1)} %all-to-all-done.3.code_ref, bf16[1536,1536]{1,0:T(8,128)(2,1)} %get-tuple-element.32.wh_ref, bf16[1536,1536]{1,0:T(8,128)(2,1)} %get-tuple-element.33.wl_ref), custom_call_target="tpu_custom_call" | custom-call | flops 14495514624 | bytes 17432588 | tf_op jit(solution)/shard_map/column/pallas_call | solution.py:226
  279.3 0.0 all-to-all-done.4
  279.3 1.6 convert_element_type.11.sums_ref
  280.9 13.5 %final.1 = f32[4096,128]{1,0:T(8,128)} custom-call(s32[3]{0:T(128)} %pad_add_fusion.where_ref, s16[128,4,4736]{2,1,0:T(4,128)(2,1)} %all-to-all-done.3.code_ref, bf16[512,1536]{1,0:T(8,128)(2,1)} %get-tuple-element.34.gh_ref, bf16[512,1536]{1,0:T(8,128)(2,1)} %get-tuple-element.35.gl_ref, f32[256,256]{1,0:T(8,128)} %get-tuple-element.36.top_ref, ...), custom_call_target="tpu_custom_call" | custom-call | flops 4831838208 | bytes 14549004 | tf_op jit(solution)/shard_map/final/pallas_call | solution.py:226
  (5 shorter events, 0.0 us)
Async XLA Ops:
  8.4 22.6 %all-to-all-start = ((f32[16,16,256]{2,1,0:T(8,128)}), f32[16,16,256]{2,1,0:T(8,128)S(1)}, u32[]{:S(2)}, u32[]{:S(2)}) async-start(f32[16,16,256]{2,1,0:T(8,128)} %bitcast.9), calls=%async_computation | async-start | bytes 524288 | tf_op jit(solution)/shard_map/all_to_all | solution.py:458
  16.8 174.7 %all-gather.2.cloned.1.call-start = ((), (), s32[]{:S(2)}) async-start(), calls=%async_computation.5 | async-start | bytes 6340608 | tf_op jit(solution)/shard_map/all_gather | solution.py:468
  31.0 0.7 collective-permute-start
  32.4 15.3 %copy-start.1 = (s32[128,64,2]{0,2,1:T(2,128)S(1)}, s32[128,64,2]{0,2,1:T(2,128)}, u32[]{:S(2)}) copy-start(s32[128,64,2]{0,2,1:T(2,128)} %param.5) | copy-start | bytes 196612
  32.4 115.5 %all-to-all-start.1 = ((bf16[128,2,64,256]{3,2,1,0:T(8,128)(2,1)}), bf16[128,2,64,256]{3,2,1,0:T(8,128)(2,1)}, u32[]{:S(2)}, u32[]{:S(2)}) async-start(bf16[128,2,64,256]{3,2,1,0:T(8,128)(2,1)} %cut_rows.1), calls=%async_computation.1 | async-start | bytes 16777216 | tf_op jit(solution)/shard_map/all_to_all | solution.py:469
  47.6 1.6 slice-start
  147.9 28.6 %all-to-all-start.2 = ((f32[128,8,256]{2,1,0:T(8,128)}), f32[128,8,256]{2,1,0:T(8,128)S(1)}, u32[]{:S(2)}, u32[]{:S(2)}) async-start(f32[128,8,256]{2,1,0:T(8,128)} %reshape.228), calls=%async_computation.2 | async-start | bytes 2097152 | tf_op jit(solution)/shard_map/all_to_all | solution.py:480
  178.1 2.2 copy-start
  180.3 67.2 %all-to-all-start.3 = ((s16[128,4,4736]{2,1,0:T(4,128)(2,1)}), s16[128,4,4736]{2,1,0:T(4,128)(2,1)}, u32[]{:S(2)}, u32[]{:S(2)}) async-start(s16[128,4,4736]{2,1,0:T(4,128)(2,1)} %copy-done), calls=%async_computation.3 | async-start | bytes 9699328 | tf_op jit(solution)/shard_map/all_to_all | solution.py:497
  247.6 31.7 %all-to-all-start.4 = ((f16[128,8,512]{2,1,0:T(8,128)(2,1)}), f16[128,8,512]{2,1,0:T(8,128)(2,1)S(1)}, u32[]{:S(2)}, u32[]{:S(2)}) async-start(f16[128,8,512]{2,1,0:T(8,128)(2,1)} %convert_bitcast_fusion), calls=%async_computation.4 | async-start | bytes 2097152 | tf_op jit(solution)/shard_map/all_to_all | solution.py:517
Sparse Core Ops, SparseCore 0:
  32.5 158.9 all-gather.1

commit v5 on v4

--- a/solution.py
+++ b/solution.py
@@ -464,7 +464,6 @@
     places = {(i, j): (i, j) for i in range(PANELS) for j in range(min(i, 2) + 1)}
     places |= {(3, 3): (0, 1), (4, 3): (7, 0), (4, 4): (7, 1)}
     places |= {(5, 3): (6, 0), (5, 4): (6, 1), (5, 5): (6, 2)}
-    cut, packed = lax.optimization_barrier((cut, packed))
     packed = lax.all_gather(packed, BOTH, axis=0, tiled=True)
     spread = lax.all_to_all(cut, BOTH, split_axis=0, concat_axis=0, tiled=True)
     later, _ = lax.optimization_barrier((parent_front, cut))

time: 302 us -> 302 us (level)
  no operation moved by 1% of the time
where the time goes in v5:
time: 302 us; the launch traced here: 301 us
  Pallas kernels  126 us (42%)
  waiting for transfers between devices  93.8 us (31%)
  starting transfers between devices  47.8 us (16%)
  between operations  13.6 us (5%)
  other arithmetic  12.3 us (4%)
  local copies, waits for them, and re-layouts  8.16 us (3%)
    pallas_call x4, Pallas kernels, whole_call(): pl.pallas_call(kernel, out_shape=out_shape, in_specs=[pl.BlockSpec(memory...  96.3 us
    all_to_all x1, waiting for transfers between devices, shards(): spread = lax.all_to_all(cut, BOTH, split_axis=0, concat_axis=0, tiled=True)  87.3 us
    all_to_all x1, starting transfers between devices, shards(): spread = lax.all_to_all(cut, BOTH, split_axis=0, concat_axis=0, tiled=True)  15.3 us
    pallas_call x1, Pallas kernels, child_sum(): pl.pallas_call(child_sum_kernel, out_shape=jax.ShapeDtypeStruct((tiles, p...  15.2 us
    pallas_call x1, Pallas kernels, cut_rows(): pl.pallas_call(cut_kernel, out_shape=jax.ShapeDtypeStruct((devices, deep,...  14.1 us
    all_to_all x1, starting transfers between devices, shards(): base = lax.all_to_all(base, BOTH, split_axis=0, concat_axis=0, tiled=True)  9.95 us
    all_to_all x1, starting transfers between devices, shards(): mine = lax.all_to_all(mine, 'col', 0, 0, tiled=True)  8.43 us
    all_to_all x1, starting transfers between devices, shards(): lax.all_to_all(to_both, BOTH, split_axis=0, concat_axis=0, tiled=True)  7.98 us
  transfers between devices with their start and end apart: 7, of which 4 were waited for; matrix products, arithmetic and copies ran while one was open for 5% of the time, Pallas kernels for 37%

profile of v5, /device:TPU:1, one launch (start us, length us, event | category | flops | bytes accessed | tf_op | source)
XLA Modules:
  0.0 301.3 jit_solution(1379969238617840438)
XLA Ops:
  6.5 1.1 slice.29
  7.7 0.7 copy.36
  8.4 8.4 %all-to-all-start = ((f32[16,16,256]{2,1,0:T(8,128)}), f32[16,16,256]{2,1,0:T(8,128)S(1)}, u32[]{:S(2)}, u32[]{:S(2)}) async-start(f32[16,16,256]{2,1,0:T(8,128)} %bitcast.9), calls=%async_computation | async-start | bytes 524288 | tf_op jit(solution)/shard_map/all_to_all | solution.py:458
  16.8 0.0 all-gather.2.cloned.1.call-start
  16.9 14.1 %cut_rows.1 = bf16[128,2,64,256]{3,2,1,0:T(8,128)(2,1)} custom-call(bf16[64,256,256]{2,1,0:T(8,128)(2,1)} %bitcast.21), custom_call_target="tpu_custom_call" | custom-call | flops 4194304 | bytes 16777216 | tf_op jit(solution)/shard_map/cut_rows/pallas_call | solution.py:172
  30.9 0.0 all-to-all-done
  31.0 0.7 collective-permute-start
  31.7 0.0 collective-permute-done
  31.7 0.6 fusion
  32.3 0.0 all-gather.2.cloned.1.call-update
  32.4 0.0 copy-start.1
  32.4 15.3 %all-to-all-start.1 = ((bf16[128,2,64,256]{3,2,1,0:T(8,128)(2,1)}), bf16[128,2,64,256]{3,2,1,0:T(8,128)(2,1)}, u32[]{:S(2)}, u32[]{:S(2)}) async-start(bf16[128,2,64,256]{3,2,1,0:T(8,128)(2,1)} %cut_rows.1), calls=%async_computation.1 | async-start | bytes 16777216 | tf_op jit(solution)/shard_map/all_to_all | solution.py:468
  47.6 0.0 slice-start
  47.7 0.0 copy-done.1
  47.7 0.1 fusion.3
  47.7 0.1 copy.22
  47.8 0.1 reshape_squeeze.16
  47.9 0.1 copy.26
  48.0 0.1 reshape_squeeze.17
  48.1 0.6 pad_add_fusion.where_ref
  48.8 0.5 add_add_fusion.target_ref
  49.3 0.0 slice-done
  49.3 0.7 copy.35
  50.0 1.3 reshape.227
  51.3 7.7 %reduce = f32[4,256,2,256]{3,2,1,0:T(2,128)S(1)} reduce(f32[4,1,256,2,1,256]{5,4,3,2,1,0:T(1,128)} %param.3, f32[]{:T(128)} %constant.67), dimensions={1,4}, to_apply=%get-tuple-element.21.reduce_sub_computation | reduce | bytes 4194308 | tf_op jit(solution)/shard_map/optimization_barrier | solution.py:469
  59.0 1.6 copy.38
  60.6 87.3 %all-to-all-done.1.child_ref = bf16[128,2,64,256]{3,2,1,0:T(8,128)(2,1)} async-done(((bf16[128,2,64,256]{3,2,1,0:T(8,128)(2,1)}), bf16[128,2,64,256]{3,2,1,0:T(8,128)(2,1)}, u32[]{:S(2)}, u32[]{:S(2)}) %all-to-all-start.1) | async-done | bytes 8388640 | tf_op jit(solution)/shard_map/all_to_all | solution.py:468
  147.9 9.9 %all-to-all-start.2 = ((f32[128,8,256]{2,1,0:T(8,128)}), f32[128,8,256]{2,1,0:T(8,128)S(1)}, u32[]{:S(2)}, u32[]{:S(2)}) async-start(f32[128,8,256]{2,1,0:T(8,128)} %reshape.227), calls=%async_computation.2 | async-start | bytes 2097152 | tf_op jit(solution)/shard_map/all_to_all | solution.py:479
  157.9 15.2 %child_sum.1.sums_ref = f32[1024,512]{1,0:T(8,128)S(1)} custom-call(s32[16,1,512]{2,1,0:T(1,128)S(1)} %add_add_fusion.target_ref, bf16[128,2,64,256]{3,2,1,0:T(8,128)(2,1)} %all-to-all-done.1.child_ref), custom_call_target="tpu_custom_call" | custom-call | flops 8589934592 | bytes 10485760 | tf_op jit(solution)/shard_map/child_sum/pallas_call | solution.py:204
  173.1 1.2 convert_bitcast_fusion
  174.3 2.2 all-to-all-done.2.base_ref
  176.5 1.6 encode.1
  178.1 0.0 copy-start
  178.1 2.2 copy-done
  180.3 8.0 %all-to-all-start.3 = ((s16[128,4,4736]{2,1,0:T(4,128)(2,1)}), s16[128,4,4736]{2,1,0:T(4,128)(2,1)}, u32[]{:S(2)}, u32[]{:S(2)}) async-start(s16[128,4,4736]{2,1,0:T(4,128)(2,1)} %copy-done), calls=%async_computation.3 | async-start | bytes 9699328 | tf_op jit(solution)/shard_map/all_to_all | solution.py:496
  188.3 3.2 %all-gather.2.cloned.1.call-done.a_ref = f32[2048,768]{1,0:T(8,128)} async-done(((f32[16,768]{1,0:T(8,128)}), f32[2048,768]{1,0:T(8,128)}) %all-gather.2.cloned.1.call-update) | async-done | bytes 6291472 | tf_op jit(solution)/shard_map/all_gather | solution.py:467
  191.5 55.0 %leading.1 = (bf16[1536,1536]{1,0:T(8,128)(2,1)}, bf16[1536,1536]{1,0:T(8,128)(2,1)}, f32[256,256]{1,0:T(8,128)}) custom-call(s32[3]{0:T(128)} %pad_add_fusion.where_ref, f32[2048,768]{1,0:T(8,128)} %all-gather.2.cloned.1.call-done.a_ref), custom_call_target="tpu_custom_call" | custom-call | flops 86973087744 | bytes 15990796 | tf_op jit(solution)/shard_map/leading/pallas_call | solution.py:226
  246.5 1.1 all-to-all-done.3.code_ref
  247.6 5.5 %all-to-all-start.4 = ((f16[128,8,512]{2,1,0:T(8,128)(2,1)}), f16[128,8,512]{2,1,0:T(8,128)(2,1)S(1)}, u32[]{:S(2)}, u32[]{:S(2)}) async-start(f16[128,8,512]{2,1,0:T(8,128)(2,1)} %convert_bitcast_fusion), calls=%async_computation.4 | async-start | bytes 2097152 | tf_op jit(solution)/shard_map/all_to_all | solution.py:516
  253.1 26.2 %column.1 = (bf16[512,1536]{1,0:T(8,128)(2,1)}, bf16[512,1536]{1,0:T(8,128)(2,1)}) custom-call(s32[3]{0:T(128)} %pad_add_fusion.where_ref, s16[128,4,4736]{2,1,0:T(4,128)(2,1)} %all-to-all-done.3.code_ref, bf16[1536,1536]{1,0:T(8,128)(2,1)} %get-tuple-element.28.wh_ref, bf16[1536,1536]{1,0:T(8,128)(2,1)} %get-tuple-element.29.wl_ref), custom_call_target="tpu_custom_call" | custom-call | flops 14495514624 | bytes 17432588 | tf_op jit(solution)/shard_map/column/pallas_call | solution.py:226
  279.3 0.0 all-to-all-done.4
  279.3 1.6 convert_element_type.11.sums_ref
  280.9 13.5 %final.1 = f32[4096,128]{1,0:T(8,128)} custom-call(s32[3]{0:T(128)} %pad_add_fusion.where_ref, s16[128,4,4736]{2,1,0:T(4,128)(2,1)} %all-to-all-done.3.code_ref, bf16[512,1536]{1,0:T(8,128)(2,1)} %get-tuple-element.30.gh_ref, bf16[512,1536]{1,0:T(8,128)(2,1)} %get-tuple-element.31.gl_ref, f32[256,256]{1,0:T(8,128)} %get-tuple-element.32.top_ref, ...), custom_call_target="tpu_custom_call" | custom-call | flops 4831838208 | bytes 14549004 | tf_op jit(solution)/shard_map/final/pallas_call | solution.py:226
  (5 shorter events, 0.0 us)
Async XLA Ops:
  8.4 22.6 %all-to-all-start = ((f32[16,16,256]{2,1,0:T(8,128)}), f32[16,16,256]{2,1,0:T(8,128)S(1)}, u32[]{:S(2)}, u32[]{:S(2)}) async-start(f32[16,16,256]{2,1,0:T(8,128)} %bitcast.9), calls=%async_computation | async-start | bytes 524288 | tf_op jit(solution)/shard_map/all_to_all | solution.py:458
  16.8 174.7 %all-gather.2.cloned.1.call-start = ((), (), s32[]{:S(2)}) async-start(), calls=%async_computation.5 | async-start | bytes 6340608 | tf_op jit(solution)/shard_map/all_gather | solution.py:467
  31.0 0.7 collective-permute-start
  32.4 15.3 %copy-start.1 = (s32[128,64,2]{0,2,1:T(2,128)S(1)}, s32[128,64,2]{0,2,1:T(2,128)}, u32[]{:S(2)}) copy-start(s32[128,64,2]{0,2,1:T(2,128)} %param.5) | copy-start | bytes 196612
  32.4 115.5 %all-to-all-start.1 = ((bf16[128,2,64,256]{3,2,1,0:T(8,128)(2,1)}), bf16[128,2,64,256]{3,2,1,0:T(8,128)(2,1)}, u32[]{:S(2)}, u32[]{:S(2)}) async-start(bf16[128,2,64,256]{3,2,1,0:T(8,128)(2,1)} %cut_rows.1), calls=%async_computation.1 | async-start | bytes 16777216 | tf_op jit(solution)/shard_map/all_to_all | solution.py:468
  47.6 1.6 slice-start
  147.9 28.6 %all-to-all-start.2 = ((f32[128,8,256]{2,1,0:T(8,128)}), f32[128,8,256]{2,1,0:T(8,128)S(1)}, u32[]{:S(2)}, u32[]{:S(2)}) async-start(f32[128,8,256]{2,1,0:T(8,128)} %reshape.227), calls=%async_computation.2 | async-start | bytes 2097152 | tf_op jit(solution)/shard_map/all_to_all | solution.py:479
  178.1 2.2 copy-start
  180.3 67.2 %all-to-all-start.3 = ((s16[128,4,4736]{2,1,0:T(4,128)(2,1)}), s16[128,4,4736]{2,1,0:T(4,128)(2,1)}, u32[]{:S(2)}, u32[]{:S(2)}) async-start(s16[128,4,4736]{2,1,0:T(4,128)(2,1)} %copy-done), calls=%async_computation.3 | async-start | bytes 9699328 | tf_op jit(solution)/shard_map/all_to_all | solution.py:496
  247.6 31.7 %all-to-all-start.4 = ((f16[128,8,512]{2,1,0:T(8,128)(2,1)}), f16[128,8,512]{2,1,0:T(8,128)(2,1)S(1)}, u32[]{:S(2)}, u32[]{:S(2)}) async-start(f16[128,8,512]{2,1,0:T(8,128)(2,1)} %convert_bitcast_fusion), calls=%async_computation.4 | async-start | bytes 2097152 | tf_op jit(solution)/shard_map/all_to_all | solution.py:516
Sparse Core Ops, SparseCore 0:
  32.5 158.9 all-gather.1
